TPU v7x, 256 devices: a whole 4x4x8 slice. The times are simulated.
256 devices in a mesh: seq: 16 (over x, z_lo), mp: 4 (over y), dp: 4 (over z_hi, core).
Axes of the slice: x: 4, y: 4, z: 8 (z_hi: 2, z_lo: 4; z = z_hi * 4 + z_lo), core: 2. Of those that a mesh axis runs over, the one named last changes fastest.
Arguments:
- block_input: bfloat16 [4, 16384, 1280], P('dp', 'seq', 'mp'), may hold values from -6 to 6
- conv_weight: bfloat16 [5, 1280, 1536], P(None, None, 'mp'), as said below
- norm_gain: float32 [1536], P('mp'), may hold values from 0.1 to 1.9
- qkv_weight: bfloat16 [1536, 2560], P(None, 'mp'), may hold values from -0.15625 to 0.15625
- encoder_grad: bfloat16 [4, 8192, 1536], P('dp', 'seq', 'mp'), may hold values from -6 to 6
Outputs:
- qkv: bfloat16 [4, 8192, 2560], P('dp', 'seq', 'mp')
- conv_grad: float32 [1280, 5, 1536], P('seq', None, 'mp')
Inputs may be any that keep to these rules, and one draw needn't show every extreme that they name: `conv_weight`: output channel o's kernel column carries a scale factor that varies with o; input channels differ in scale.
All inputs are finite; a program needn't handle non-finite values.
Results may differ from a plain program's by a relative error of at most 0.019.
Values may be sent and summed in bfloat16 or wider, within the bound.
A program may use at most 64 MiB of HBM per device.

v0:
```python
import jax
import jax.numpy as jnp
from jax import lax
from jax.sharding import PartitionSpec as P

KW = 5


def padded_2(value, sides, width):
    for axis, dim in sides:
        peers, length = (lax.axis_size(axis), value.shape[dim])
        up = [(i, (i + 1) % peers) for i in range(peers - 1)]
        down = [(j, i) for i, j in up]
        last = lax.slice_in_dim(value, length - width, length, axis=dim)
        initial = lax.slice_in_dim(value, 0, width, axis=dim)
        before = lax.ppermute(last, axis, up)
        after = lax.ppermute(initial, axis, down)
        value = jnp.concatenate([before, value, after], axis=dim)
    return value


def gelu_value(v):
    u = 0.7978845608 * (v + 0.044715 * v * v * v)
    return 0.5 * v * (1.0 + jnp.tanh(u))


def gelu_slope(v):
    u = 0.7978845608 * (v + 0.044715 * v * v * v)
    th = jnp.tanh(u)
    return 0.5 * (1.0 + th) + 0.5 * v * (1.0 - th * th) * 0.7978845608 * (1.0 + 0.134145 * v * v)


def on_device(block_input, conv_weight, norm_gain, qkv_weight, encoder_grad):
    local_input = block_input[0]
    length = local_input.shape[0]
    rimmed = padded_2(local_input, (("seq", 0),), 2)
    padded = lax.all_gather(rimmed, "mp", axis=1, tiled=True)
    pre = jnp.zeros((length, conv_weight.shape[2]), jnp.float32)
    for k in range(KW):
        pre = pre + jnp.dot(
            padded[k : k + length], conv_weight[k], preferred_element_type=jnp.float32
        )
    act = gelu_value(pre)
    encoded = (0.5 * (act[0::2] + act[1::2])).astype(jnp.bfloat16)
    values = encoded.astype(jnp.float32)
    channels = values.shape[1] * lax.axis_size("mp")
    sums, squares = lax.psum((jnp.sum(values, axis=1), jnp.sum(values * values, axis=1)), "mp")
    mean = sums[:, None] / channels
    var = squares[:, None] / channels - mean * mean
    normalized = ((values - mean) * lax.rsqrt(var + 1e-05) * norm_gain).astype(jnp.bfloat16)
    qkv = jnp.dot(
        lax.all_gather(normalized, "mp", axis=1, tiled=True),
        qkv_weight,
        preferred_element_type=jnp.float32,
    ).astype(jnp.bfloat16)
    spread = jnp.repeat(encoder_grad[0].astype(jnp.float32), 2, axis=0)
    pre_grad = (gelu_slope(pre) * 0.5 * spread).astype(jnp.bfloat16)
    terms = [
        lax.dot_general(
            padded[k : k + length],
            pre_grad,
            (((0,), (0,)), ((), ())),
            preferred_element_type=jnp.float32,
        )
        for k in range(KW)
    ]
    share = lax.psum_scatter(
        jnp.stack(terms, axis=1).astype(jnp.bfloat16), "seq", scatter_dimension=0, tiled=True
    )
    conv_grad = lax.psum(share, "dp").astype(jnp.float32)
    return (qkv[None], conv_grad)


def solution(mesh):
    return jax.shard_map(
        on_device,
        mesh=mesh,
        in_specs=(
            P("dp", "seq", "mp"),
            P(None, None, "mp"),
            P("mp"),
            P(None, "mp"),
            P("dp", "seq", "mp"),
        ),
        out_specs=(P("dp", "seq", "mp"), P("seq", None, "mp")),
        check_vma=False,
    )
```

profile of v0, /device:TPU:1, one launch (start us, length us, event | category | flops | bytes accessed | tf_op | source)
XLA Modules:
  0.0 311.2 jit_solution(616916708142689634)
XLA Ops:
  9.7 5.0 %collective-permute-start = (bf16[2,320]{0,1:T(8,128)(2,1)S(1)}, bf16[2,320]{0,1:T(8,128)(2,1)S(1)}, u32[]{:S(2)}, u32[]{:S(2)}) collective-permute-start(bf16[2,320]{0,1:T(8,128)(2,1)S(1)} %get-tuple-element.10), channel_id=1, source_target_pairs={{0,16},{16,32},{32,48},{48,64},{64,80},{80,96},{96,112},{112,128},... | collective-permute-start | bytes 3848 | tf_op jit(solution)/shard_map/ppermute | solution.py:16
  16.2 2.3 concatenate.3
  19.2 2.2 reshape.20
  21.5 1.9 copy.8
  23.3 44.5 %all-gather.3.cloned.1.call-done = bf16[1028,1280]{0,1:T(8,128)(2,1)} async-done(((bf16[1028,320]{0,1:T(8,128)(2,1)}), bf16[1028,1280]{0,1:T(8,128)(2,1)}) %all-gather.3.cloned.1.call-update) | async-done | bytes 2631696 | tf_op jit(solution)/shard_map/all_gather | solution.py:37
  67.9 3.7 %fusion.14 = f32[1024,384]{0,1:T(8,128)S(1)} fusion(bf16[1028,1280]{0,1:T(8,128)(2,1)} %all-gather.3.cloned.1.call-done, bf16[5,1280,384]{2,1,0:T(8,128)(2,1)} %param.6), kind=kOutput, calls=%fused_computation.21 | convolution fusion | flops 1006632960 | bytes 5177344 | tf_op jit(solution)/shard_map/dot_general | solution.py:40
  71.6 2.7 fusion.17
  74.3 2.7 fusion.20
  76.9 2.4 fusion.23
  79.4 5.0 %fusion.32 = (bf16[1024,384]{0,1:T(8,128)(2,1)S(1)}, f32[1024,384]{0,1:T(8,128)}) fusion(f32[1024,384]{0,1:T(8,128)S(1)} %copy.8, bf16[5,1280,384]{2,1,0:T(8,128)(2,1)} %param.6, bf16[1028,1280]{0,1:T(8,128)(2,1)S(1)} %copy-done.3, f32[1024,384]{0,1:T(8,128)S(1)} %fusion.14, f32[1024,384]{0,1:T(8,128)S(1)} %fusion.17, f32[1024,384]{0,1:T(8,128)S(1)} %fusion.23, ...), kind=kOutput, calls=%fused_computation.39 | convolution fusion | flops 1016463360 | bytes 13828096 | tf_op jit(solution)/shard_map/dot_general | solution.py:40
  84.3 2.5 fusion.1
  86.8 2.8 fusion.3
  89.6 2.5 fusion.5
  92.1 2.5 fusion.7
  94.7 2.5 fusion.9
  97.3 27.9 %slice.68 = f32[512,384]{0,1:T(8,128)S(1)} slice(f32[1024,384]{0,1:T(8,128)} %get-tuple-element.8), slice={[1:1024:2], [0:384:1]} | slice | bytes 1572864 | tf_op jit(solution)/shard_map/slice | solution.py:44
  125.2 27.9 %slice.67 = f32[512,384]{0,1:T(8,128)S(1)} slice(f32[1024,384]{0,1:T(8,128)} %get-tuple-element.8), slice={[0:1024:2], [0:384:1]} | slice | bytes 1572864 | tf_op jit(solution)/shard_map/slice | solution.py:44
  154.0 7.3 %all-reduce = (f32[512]{0:T(512)S(1)}, f32[512]{0:T(512)S(1)}) all-reduce(f32[512]{0:T(512)S(1)} %get-tuple-element.3, f32[512]{0:T(512)S(1)} %get-tuple-element.2), channel_id=1, replica_groups=mesh['seq'=16,'mp'=4,'dp'=4] {'mp'}, use_global_device_ids=true, to_apply=%region_3.0 | all-reduce | flops 1024 | bytes 8192 | tf_op jit(solution)/shard_map/psum | solution.py:47
  161.3 1.9 fusion.50
  163.3 51.7 %reduce-scatter.2.cloned.1.call-done = bf16[80,5,384]{2,0,1:T(8,128)(2,1)} async-done(((bf16[1280,5,384]{2,0,1:T(8,128)(2,1)}), bf16[80,5,384]{2,0,1:T(8,128)(2,1)}) %reduce-scatter.2.cloned.1.call-update) | async-done | bytes 307216 | tf_op jit(solution)/shard_map/reduce_scatter | solution.py:67
  215.1 29.0 %all-gather.5.cloned.1.call-done = bf16[512,1536]{0,1:T(8,128)(2,1)} async-done(((bf16[512,384]{0,1:T(8,128)(2,1)}), bf16[512,1536]{0,1:T(8,128)(2,1)}) %all-gather.5.cloned.1.call-update) | async-done | bytes 1572880 | tf_op jit(solution)/shard_map/all_gather | solution.py:52
  244.0 3.7 %fusion.33 = bf16[1,512,640]{2,1,0:T(8,128)(2,1)} fusion(bf16[512,1536]{0,1:T(8,128)(2,1)} %all-gather.5.cloned.1.call-done, bf16[1536,640]{1,0:T(8,128)(2,1)S(1)} %copy-done), kind=kOutput, calls=%fused_computation.43 | convolution fusion | flops 1006960640 | bytes 4194304 | tf_op jit(solution)/shard_map/dot_general | solution.py:51
  247.7 55.1 %all-reduce.3.cloned.1.call-done = bf16[80,5,384]{2,0,1:T(8,128)(2,1)} async-done(((bf16[80,5,384]{2,0,1:T(8,128)(2,1)}), bf16[80,5,384]{2,0,1:T(8,128)(2,1)}) %all-reduce.3.cloned.1.call-update) | async-done | bytes 307216 | tf_op jit(solution)/shard_map/psum | solution.py:70
  302.8 1.8 convert_element_type.32
  (24 shorter events, 5.7 us)
Async XLA Ops:
  7.2 236.9 %copy-start = (bf16[1536,640]{1,0:T(8,128)(2,1)S(1)}, bf16[1536,640]{1,0:T(8,128)(2,1)}, u32[]{:S(2)}) copy-start(bf16[1536,640]{1,0:T(8,128)(2,1)} %param.8) | copy-start | bytes 5898244
  7.2 11.4 %copy-start.1 = (bf16[1,512,384]{2,1,0:T(8,128)(2,1)S(1)}, bf16[1,512,384]{2,1,0:T(8,128)(2,1)}, u32[]{:S(2)}) copy-start(bf16[1,512,384]{2,1,0:T(8,128)(2,1)} %param.9) | copy-start | bytes 1179652
  7.2 60.7 %all-gather.3.cloned.1.call-start = ((), (), s32[]{:S(2)}) async-start(), calls=%async_computation.1 | async-start | bytes 3686400 | tf_op jit(solution)/shard_map/all_gather | solution.py:37
  8.4 6.3 %collective-permute-start.1 = (bf16[2,320]{0,1:T(8,128)(2,1)S(1)}, bf16[2,320]{0,1:T(8,128)(2,1)S(1)}, u32[]{:S(2)}, u32[]{:S(2)}) collective-permute-start(bf16[2,320]{0,1:T(8,128)(2,1)S(1)} %get-tuple-element.9), channel_id=1, source_target_pairs={{16,0},{32,16},{48,32},{64,48},{80,64},{96,80},{112,96},{128,112},... | collective-permute-start | bytes 3848 | tf_op jit(solution)/shard_map/ppermute | solution.py:17
  9.7 6.5 %collective-permute-start = (bf16[2,320]{0,1:T(8,128)(2,1)S(1)}, bf16[2,320]{0,1:T(8,128)(2,1)S(1)}, u32[]{:S(2)}, u32[]{:S(2)}) collective-permute-start(bf16[2,320]{0,1:T(8,128)(2,1)S(1)} %get-tuple-element.10), channel_id=1, source_target_pairs={{0,16},{16,32},{32,48},{48,64},{64,80},{80,96},{96,112},{112,128},... | collective-permute-start | bytes 3848 | tf_op jit(solution)/shard_map/ppermute | solution.py:16
  18.6 196.5 %reduce-scatter.2.cloned.1.call-start = ((), (), s32[]{:S(2)}) async-start(), calls=%async_computation.3 | async-start | bytes 5222400 | tf_op jit(solution)/shard_map/reduce_scatter | solution.py:67
  67.9 3.7 %copy-start.3 = (bf16[1028,1280]{0,1:T(8,128)(2,1)S(1)}, bf16[1028,1280]{0,1:T(8,128)(2,1)}, u32[]{:S(2)}) copy-start(bf16[1028,1280]{0,1:T(8,128)(2,1)} %all-gather.3.cloned.1.call-done) | copy-start | bytes 7895044
  97.3 64.1 %copy-start.2 = (f32[384]{0:T(512)S(1)}, f32[384]{0:T(512)}, u32[]{:S(2)}) copy-start(f32[384]{0:T(512)} %param.7) | copy-start | bytes 4612
  97.3 146.8 %all-gather.5.cloned.1.call-start = ((), (), s32[]{:S(2)}) async-start(), calls=%async_computation.2 | async-start | bytes 1966080 | tf_op jit(solution)/shard_map/all_gather | solution.py:52
  163.2 139.6 %all-reduce.3.cloned.1.call-start = ((), (), s32[]{:S(2)}) async-start(), calls=%async_computation.4 | async-start | bytes 614400 | tf_op jit(solution)/shard_map/psum | solution.py:70
Sparse Core Ops, SparseCore 0:
  18.7 49.1 all-gather.2
  97.4 117.6 reduce-scatter.1
  217.4 26.5 all-gather.4
  246.5 56.2 all-reduce.2
where the time goes:
time: 312 us; the launch traced here: 311 us
  waiting for transfers between devices  182 us (58%)
  local copies, waits for them, and re-layouts  63.9 us (20%)
  matrix products  33 us (11%)
  between operations  13.9 us (4%)
  blocking collectives  7.32 us (2%)
  starting transfers between devices  6.45 us (2%)
  other arithmetic  4.71 us (2%)
    slice x2, local copies, waits for them, and re-layouts, on_device(): encoded = (0.5 * (act[0::2] + act[1::2])).astype(jnp.bfloat16)  55.7 us
    psum x1, waiting for transfers between devices, on_device(): conv_grad = lax.psum(share, 'dp').astype(jnp.float32)  55.1 us
    reduce_scatter x1, waiting for transfers between devices, on_device(): lax.psum_scatter(jnp.stack(terms, axis=1).astype(jnp.bfloat16), 'seq', sc...  51.7 us
    all_gather x1, waiting for transfers between devices, on_device(): padded = lax.all_gather(rimmed, 'mp', axis=1, tiled=True)  44.5 us
    all_gather x1, waiting for transfers between devices, on_device(): lax.all_gather(normalized, 'mp', axis=1, tiled=True)  29 us
    dot_general x5, matrix products, on_device(): jnp.dot(padded[k:k + length], conv_weight[k], preferred_element_type=jnp....  16.4 us
    dot_general x5, matrix products, on_device(): lax.dot_general(padded[k:k + length], pre_grad, (((0,), (0,)), ((), ())),...  12.9 us
    psum x1, blocking collectives, on_device(): lax.psum((jnp.sum(values, axis=1), jnp.sum(values * values, axis=1)), 'mp')  7.32 us
  transfers between devices with their start and end apart: 6, of which 5 were waited for; matrix products, arithmetic and copies ran while one was open for 22% of the time, Pallas kernels for 0%

commit v1 on v0

v1 whole, which is shorter than its diff:
```python
import jax
import jax.numpy as jnp
from jax import lax
from jax.experimental import pallas as pl
from jax.experimental.pallas import tpu as pltpu
from jax.sharding import PartitionSpec as P

MESH = pl.DeviceIdType.MESH
BF16, F32 = jnp.bfloat16, jnp.float32
KW = 5
T = 1024
R = 512
CB = 320
O = 384
OT = O // 128
C = 4 * CB
N = KW * O
W2 = 1024
Q = 640
TB = 256
NB = T // TB
XB = 320
ZB = 80
PIECE = 512
Y0 = 8

OWN_R, OWN_L, FWD_R, FWD_L = 0, 4, 8, 12
EDGE_UP, EDGE_DOWN, RIM, GAIN = 16, 17, 17, 20
ENC_R, ENC_L, EFWD_R, EFWD_L = 24, 26, 28, 29
SWAP = 30
X1R, X1L, X2R, X2L = 34, 35, 36, 38
ZUP, ZDN, DPG = 40, 44, 47
COPIES = 51


def kernel(
    xt_hbm, edge_hbm, w_hbm, gain_hbm, qw_hbm, eg_hbm, qkv_hbm, cg_hbm,
    xt, rim, wcat, gain, qw, eg, xrow, yb, pgb, pgcat, enc, norm, qout,
    psend, precv, gown, x1l, x1r, x2l, x2r, zb, zru, zrd, zsu, zsd, fin, cgo,
    lsem, ssem, rsem,
):
    seq, mp, dp = lax.axis_index("seq"), lax.axis_index("mp"), lax.axis_index("dp")
    x, zl = seq // 4, seq % 4
    zh, core = dp // 2, dp % 2
    z = zh * 4 + zl

    def at(s=None, m=None, d=None):
        return {"seq": seq if s is None else s, "mp": mp if m is None else m, "dp": dp if d is None else d}

    def z_at(zn):
        return at(s=x * 4 + zn % 4, d=(zn // 4) * 2 + core)

    y_right, y_left = at(m=(mp + 1) % 4), at(m=(mp + 3) % 4)
    s_up, s_down = at(s=(seq + 1) % 16), at(s=(seq + 15) % 16)
    x_right, x_left = at(s=(seq + 4) % 16), at(s=(seq + 12) % 16)
    z_up, z_down = z_at((z + 1) % 8), z_at((z + 7) % 8)
    partner = at(d=zh * 2 + 1 - core)
    far = [at(d=(1 - zh) * 2 + core), at(d=(1 - zh) * 2 + 1 - core)]

    local = []

    def load(src, dst):
        copy = pltpu.make_async_copy(src, dst, lsem.at[len(local)])
        copy.start()
        local.append(copy)
        return copy

    own_rows = pl.ds(pl.multiple_of(mp * CB, CB), CB)
    own_x = load(xt_hbm, xt.at[own_rows])
    loads = [load(w_hbm.at[k], wcat.at[:, pl.ds(k * O, O)]) for k in range(KW)]
    eg_load = load(eg_hbm, eg)
    gain_load = load(gain_hbm, gain.at[mp])
    qw_load = load(qw_hbm, qw)

    barrier = pltpu.get_barrier_semaphore()
    peers = [y_right, y_left, at(m=(mp + 2) % 4), s_up, s_down, x_right, x_left, z_up, z_down, partner] + far
    for peer in peers:
        pl.semaphore_signal(barrier, inc=1, device_id=peer, device_id_type=MESH)
    pl.semaphore_wait(barrier, len(peers))

    sent = []

    def remote(src, dst, i, peer):
        return pltpu.make_async_remote_copy(
            src_ref=src, dst_ref=dst, send_sem=ssem.at[i], recv_sem=rsem.at[i], device_id=peer, device_id_type=MESH
        )

    def send(src, dst, i, peer):
        copy = remote(src, dst, i, peer)
        copy.start()
        sent.append(copy)

    def arrived(dst, i):
        remote(dst, dst, i, y_right).wait_recv()

    def block(owner, half, tb):
        first = owner * CB + (0 if half is None else half * (CB // 2))
        size = CB if half is None else CB // 2
        return xt.at[pl.ds(pl.multiple_of(first, CB // 2), size), pl.ds(tb * TB, TB)]

    m_left, m_right, m_far = (mp + 3) % 4, (mp + 1) % 4, (mp + 2) % 4

    def send_own(tb):
        src = xt_hbm.at[:, pl.ds(tb * TB, TB)]
        send(src, block(mp, None, tb), OWN_R + tb, y_right)
        send(src, block(mp, None, tb), OWN_L + tb, y_left)

    def forward(tb):
        arrived(block(m_left, None, tb), OWN_R + tb)
        send(block(m_left, 0, tb), block(m_left, 0, tb), FWD_R + tb, y_right)
        arrived(block(m_right, None, tb), OWN_L + tb)
        send(block(m_right, 1, tb), block(m_right, 1, tb), FWD_L + tb, y_left)

    def complete(tb):
        arrived(block(m_far, 0, tb), FWD_R + tb)
        arrived(block(m_far, 1, tb), FWD_L + tb)

    send(edge_hbm, rim.at[mp, pl.ds(0, 16)], EDGE_UP, s_up)
    send(edge_hbm, rim.at[mp, pl.ds(16, 16)], EDGE_DOWN, s_down)
    send_own(0)
    for d in (1, 2, 3):
        send(gain_hbm, gain.at[mp], GAIN + d, at(m=(mp + d) % 4))
    send_own(1)
    arrived(rim.at[mp, pl.ds(0, 16)], EDGE_UP)
    arrived(rim.at[mp, pl.ds(16, 16)], EDGE_DOWN)
    for d in (1, 2, 3):
        send(rim.at[mp], rim.at[mp], RIM + d, at(m=(mp + d) % 4))
    own_x.wait()

    def tap_products(tb):
        xrow[...] = xt[:, tb * TB : (tb + 1) * TB].T

        def tile(n, carry):
            cols = pl.ds(pl.multiple_of(n * 256, 256), 256)
            y = jnp.dot(xrow[...], wcat[:, cols], preferred_element_type=F32)
            yb[2 * n, pl.ds(Y0 + tb * TB, TB), :] = y[:, :128]
            yb[2 * n + 1, pl.ds(Y0 + tb * TB, TB), :] = y[:, 128:]
            return carry

        lax.fori_loop(0, N // 256, tile, 0)
        y = jnp.dot(xrow[...], wcat[:, N - 128 :], preferred_element_type=F32)
        yb[N // 128 - 1, pl.ds(Y0 + tb * TB, TB), :] = y

    def rim_products():
        for d in (1, 2, 3):
            owner = (mp + 4 - d) % 4
            arrived(rim.at[owner], RIM + d)
        before = jnp.where(seq > 0, 1.0, 0.0).astype(F32)
        after = jnp.where(seq < 15, 1.0, 0.0).astype(F32)

        def tile(n, carry):
            cols = pl.ds(pl.multiple_of(n * 128, 128), 128)
            y = jnp.zeros((32, 128), F32)
            for m in range(4):
                y += jnp.dot(rim[m][:, :CB], wcat[m * CB : (m + 1) * CB, cols], preferred_element_type=F32)
            yb[n, pl.ds(0, 8), :] = y[0:8] * before
            yb[n, pl.ds(Y0 + T, 8), :] = y[16:24] * after
            return carry

        lax.fori_loop(0, N // 128, tile, 0)

    def gelu(v):
        v2 = v * v
        th = jnp.tanh(v * (0.7978845608 + (0.7978845608 * 0.044715) * v2))
        half = 0.5 + 0.5 * th
        slope = half + 0.5 * v * (1.0 - th * th) * (0.7978845608 + (0.7978845608 * 0.134145) * v2)
        return v * half, slope

    def pre(o, row, rows, stride):
        taps = [yb[k * OT + o, pl.ds(row + k - 2, rows, stride=stride), :] for k in range(KW)]
        return taps[0] + taps[1] + taps[2] + taps[3] + taps[4]

    STEP = 32

    def activations(first, count):
        def rows_of(i, carry):
            j = pl.multiple_of(first + i * STEP, STEP)
            for o in range(OT):
                lanes = pl.ds(o * 128, 128)
                act_e, slope_e = gelu(pre(o, Y0 + 2 * j, STEP, 2))
                act_o, slope_o = gelu(pre(o, Y0 + 2 * j + 1, STEP, 2))
                g = 0.5 * eg[pl.ds(j, STEP), lanes].astype(F32)
                enc[mp, pl.ds(j, STEP), lanes] = (0.5 * (act_e + act_o)).astype(BF16)
                pgb[o, pl.ds(Y0 + 2 * j, STEP, stride=2), :] = slope_e * g
                pgb[o, pl.ds(Y0 + 2 * j + 1, STEP, stride=2), :] = slope_o * g
            return carry

        lax.fori_loop(0, count // STEP, rows_of, 0)

    def rim_gradients():
        before = jnp.where(seq > 0, 0.5, 0.0).astype(F32)
        after = jnp.where(seq < 15, 0.5, 0.0).astype(F32)
        rims = rim[mp]
        for o in range(OT):
            lanes = slice(o * 128, (o + 1) * 128)
            for row, g in ((Y0 - 2, rims[9:10, lanes].astype(F32) * before), (Y0 + T, rims[24:25, lanes].astype(F32) * after)):
                for r in (row, row + 1):
                    slope = gelu(pre(o, r, 1, 1))[1]
                    pgb[o, pl.ds(r, 1), :] = slope * g

    PSTEP = 64

    def gradient_columns():
        def rows_of(i, carry):
            s = pl.multiple_of(i * PSTEP, PSTEP)
            for k in range(KW):
                for o in range(OT):
                    pgcat[pl.ds(s, PSTEP), (k * OT + o) * 128 : (k * OT + o + 1) * 128] = pgb[
                        o, pl.ds(Y0 + s + 2 - k, PSTEP), :
                    ].astype(BF16)
            pgcat[pl.ds(s, PSTEP), N:] = jnp.zeros((PSTEP, 128), BF16)
            return carry

        lax.fori_loop(0, T // PSTEP, rows_of, 0)

    for copy in loads:
        copy.wait()
    forward(0)
    send_own(2)
    complete(0)
    tap_products(0)
    forward(1)
    send_own(3)
    rim_products()
    eg_load.wait()
    complete(1)
    tap_products(1)
    activations(0, 224)
    forward(2)
    forward(3)
    complete(2)
    tap_products(2)
    activations(224, 128)
    complete(3)
    tap_products(3)
    activations(352, 160)
    rim_gradients()

    def half_rows(owner, e):
        return enc.at[owner, pl.ds(e * (R // 2), R // 2)]

    send(half_rows(mp, 0), half_rows(mp, 0), ENC_R, y_right)
    send(half_rows(mp, 1), half_rows(mp, 1), ENC_L + 1, y_left)
    send(half_rows(mp, 1), half_rows(mp, 1), ENC_R + 1, y_right)
    send(half_rows(mp, 0), half_rows(mp, 0), ENC_L, y_left)
    gradient_columns()

    def products(xb, column, write):
        rows = pl.ds(pl.multiple_of(xb * XB, XB), XB)

        def tile(n, carry):
            cols = pl.ds(pl.multiple_of(column + n * 256, 256), 256)
            write(n, jnp.dot(xt[rows, :], pgcat[:, cols], preferred_element_type=F32))
            return carry

        lax.fori_loop(0, W2 // 256, tile, 0)

    def theirs(step, xb):
        def write(n, value):
            psend[xb, :, pl.ds(pl.multiple_of(n * 256, 256), 256)] = value.astype(BF16)

        products(xb, (1 - core) * W2, write)
        send(psend.at[xb], precv.at[xb], SWAP + step, partner)

    def ours(step, xb):
        arrived(precv.at[xb], SWAP + step)

        def write(n, value):
            cols = pl.ds(pl.multiple_of(n * 256, 256), 256)
            gown[xb, :, cols] = (value + precv[xb, :, cols].astype(F32)).astype(BF16)

        products(xb, core * W2, write)

    top, bottom = pl.ds(0, XB // 2), pl.ds(XB // 2, XB // 2)
    xf, xr, xl = (x + 2) % 4, (x + 1) % 4, (x + 3) % 4

    def add_rows(dst, src, rows):
        for r in range(0, rows, 32):
            dst[pl.ds(r, 32), :] = (dst[pl.ds(r, 32), :].astype(F32) + src[pl.ds(r, 32), :].astype(F32)).astype(BF16)

    theirs(0, xf)
    theirs(1, xr)
    ours(0, xf)
    send(gown.at[xf, top], x1l, X1R, x_right)
    send(gown.at[xf, bottom], x1r, X1L, x_left)
    theirs(2, xl)
    ours(1, xr)
    send(gown.at[xr, bottom], x2l.at[bottom], X2R + 1, x_right)
    arrived(half_rows(m_left, 0), ENC_R)
    send(half_rows(m_left, 0), half_rows(m_left, 0), EFWD_R, y_right)
    arrived(half_rows(m_right, 1), ENC_L + 1)
    send(half_rows(m_right, 1), half_rows(m_right, 1), EFWD_L, y_left)
    theirs(3, x)
    ours(2, xl)
    send(gown.at[xl, top], x2r.at[top], X2L, x_left)
    arrived(x1l, X1R)
    add_rows(gown.at[xr, top], x1l, XB // 2)
    send(gown.at[xr, top], x2l.at[top], X2R, x_right)
    arrived(x1r, X1L)
    add_rows(gown.at[xl, bottom], x1r, XB // 2)
    send(gown.at[xl, bottom], x2r.at[bottom], X2L + 1, x_left)
    ours(3, x)

    arrived(half_rows(m_left, 1), ENC_R + 1)
    arrived(half_rows(m_right, 0), ENC_L)
    arrived(half_rows(m_far, 0), EFWD_R)
    arrived(half_rows(m_far, 1), EFWD_L)
    gain_load.wait()
    for d in (1, 2, 3):
        arrived(gain.at[(mp + 4 - d) % 4], GAIN + d)

    def normalize(i, carry):
        rows = pl.ds(pl.multiple_of(i * 32, 32), 32)
        values = [enc[m, rows, :].astype(F32) for m in range(4)]
        total = jnp.sum(values[0] + values[1] + values[2] + values[3], axis=1, keepdims=True)
        square = jnp.sum(sum(v * v for v in values), axis=1, keepdims=True)
        mean = total / (4 * O)
        scale = lax.rsqrt(square / (4 * O) - mean * mean + 1e-05)
        for m in range(4):
            norm[rows, m * O : (m + 1) * O] = ((values[m] - mean) * scale * gain[m]).astype(BF16)
        return carry

    lax.fori_loop(0, R // 32, normalize, 0)
    qw_load.wait()

    def project(i, carry):
        rows = pl.ds(pl.multiple_of(i * 128, 128), 128)
        qout[rows, :] = jnp.dot(norm[rows, :], qw[...], preferred_element_type=F32).astype(BF16)
        return carry

    lax.fori_loop(0, R // 128, project, 0)
    qkv_store = load(qout, qkv_hbm)

    for half, rows in ((0, top), (1, bottom)):
        arrived(x2l.at[rows], X2R + half)
        arrived(x2r.at[rows], X2L + half)
    for g in range(4):
        for r in range(0, ZB, 16):
            rows = pl.ds(g * ZB + r, 16)
            zb[g, pl.ds(r, 16), :] = (
                gown[x, rows, :].astype(F32) + x2l[rows, :].astype(F32) + x2r[rows, :].astype(F32)
            ).astype(BF16)

    def piece(zn, lane, width):
        return zb.at[zn % 4, :, pl.ds(pl.multiple_of((zn // 4) * PIECE + lane, 256), width)]

    def pass_on(step, zn, received, buffer, lane, i, peer):
        width = PIECE // 2 if step == 1 else PIECE
        src = piece(zn, 0, PIECE)
        if step == 1:
            arrived(received.at[0, :, pl.ds(lane, width)], i)
            other = PIECE // 2 - lane
            buffer[step, :, pl.ds(other, width)] = src[:, pl.ds(other, width)]
        else:
            lane = 0
            arrived(received.at[step - 1], i + step - 1)
        cols = pl.ds(lane, width)
        buffer[step, :, cols] = (src[:, cols].astype(F32) + received[step - 1, :, cols].astype(F32)).astype(BF16)
        send(buffer.at[step], received.at[step], i + step, peer)

    zf = (z + 4) % 8
    half = PIECE // 2
    send(piece(zf, 0, half), zru.at[0, :, pl.ds(0, half)], ZUP, z_up)
    send(piece(zf, half, half), zrd.at[0, :, pl.ds(half, half)], ZDN, z_down)
    for step in (1, 2, 3):
        pass_on(step, (z + 4 - step) % 8, zru, zsu, 0, ZUP, z_up)
        pass_on(step, (z + 4 + step) % 8, zrd, zsd, half, ZDN, z_down)
    arrived(zru.at[3], ZUP + 3)
    arrived(zrd.at[3], ZDN + 3)
    mine = piece(z, 0, PIECE)
    fin[dp] = (mine[...].astype(F32) + zru[3].astype(F32) + zrd[3].astype(F32)).astype(BF16)
    for i, peer in enumerate([partner] + far):
        send(fin.at[dp], fin.at[dp], DPG + 1 + i, peer)
    for i, d in enumerate((zh * 2 + 1 - core, (1 - zh) * 2 + core, (1 - zh) * 2 + 1 - core)):
        arrived(fin.at[d], DPG + 1 + i)
    for i in range(N // 128):
        owner = (i % 8) // 4 * 2 + i // 8
        lane = (i % 4) * 128
        cgo[i // OT, :, pl.ds((i % OT) * 128, 128)] = fin[owner, :, lane : lane + 128].astype(F32)
    cg_store = load(cgo, cg_hbm)
    for copy in sent:
        copy.wait_send()
    qkv_store.wait()
    cg_store.wait()


def on_device(block_input, conv_weight, norm_gain, qkv_weight, encoder_grad):
    xin, eg = block_input[0], encoder_grad[0]
    edge = jnp.concatenate(
        [
            jnp.pad(jnp.concatenate([xin[:4], xin[-4:]]), ((0, 0), (0, O - CB))),
            eg[:1],
            eg[-1:],
            jnp.zeros((6, O), BF16),
        ]
    )
    any_ = pl.BlockSpec(memory_space=pl.ANY)
    v = pltpu.VMEM
    qkv, grad = pl.pallas_call(
        kernel,
        name="block",
        out_shape=(jax.ShapeDtypeStruct((R, Q), BF16), jax.ShapeDtypeStruct((KW, ZB, O), F32)),
        in_specs=[any_] * 6,
        out_specs=(any_, any_),
        scratch_shapes=[
            v((C, T), BF16), v((4, 32, O), BF16), v((C, N), BF16), v((4, 1, O), F32), v((4 * O, Q), BF16), v((R, O), BF16),
            v((TB, C), BF16), v((N // 128, T + 16, 128), F32), v((OT, T + 16, 128), F32), v((T, 2 * W2), BF16),
            v((4, R, O), BF16), v((R, 4 * O), BF16), v((R, Q), BF16),
            v((4, XB, W2), BF16), v((4, XB, W2), BF16), v((4, XB, W2), BF16),
            v((XB // 2, W2), BF16), v((XB // 2, W2), BF16), v((XB, W2), BF16), v((XB, W2), BF16),
            v((4, ZB, W2), BF16), v((4, ZB, PIECE), BF16), v((4, ZB, PIECE), BF16), v((4, ZB, PIECE), BF16), v((4, ZB, PIECE), BF16),
            v((4, ZB, PIECE), BF16), v((KW, ZB, O), F32),
            pltpu.SemaphoreType.DMA((12,)), pltpu.SemaphoreType.DMA((COPIES,)), pltpu.SemaphoreType.DMA((COPIES,)),
        ],
        compiler_params=pltpu.CompilerParams(collective_id=0, has_side_effects=True, vmem_limit_bytes=60 * 2**20),
    )(xin.T, edge, conv_weight, norm_gain.reshape(1, O), qkv_weight, eg)
    return qkv[None], grad.transpose(1, 0, 2)


def solution(mesh):
    return jax.shard_map(
        on_device,
        mesh=mesh,
        in_specs=(
            P("dp", "seq", "mp"),
            P(None, None, "mp"),
            P("mp"),
            P(None, "mp"),
            P("dp", "seq", "mp"),
        ),
        out_specs=(P("dp", "seq", "mp"), P("seq", None, "mp")),
        check_vma=False,
    )
```

time: 312 us -> 113 us (0.36)
  waiting for transfers between devices: 182 us -> 0 us
  Pallas kernels: 0 us -> 104 us
  local copies, waits for them, and re-layouts: 63.9 us -> 7.17 us
  matrix products: 33 us -> 0 us
  between operations: 13.9 us -> 0.66 us
  blocking collectives: 7.32 us -> 0 us
  starting transfers between devices: 6.45 us -> 0 us
  other arithmetic: 4.71 us -> 0.71 us
    pallas_call x0 -> x1, Pallas kernels: none -> 104 us  [on_device(): pl.pallas_call(kernel, name='block', out_shape=(jax.ShapeDtypeStruct((R,...]
    all_gather x2 -> x0, waiting for transfers between devices: 73.5 us -> none  [the longest x1 44.5 us: on_device(): padded = lax.all_gather(rimmed, 'mp', axis=1, tiled=True)]
    slice x3 -> x2, local copies, waits for them, and re-layouts: 56.9 us -> 1.73 us  [the longest x1 1.02 us: on_device(): xin[:4]]
    psum x1 -> x0, waiting for transfers between devices: 55.1 us -> none  [on_device(): conv_grad = lax.psum(share, 'dp').astype(jnp.float32)]
    reduce_scatter x1 -> x0, waiting for transfers between devices: 51.7 us -> none  [on_device(): lax.psum_scatter(jnp.stack(terms, axis=1).astype(jnp.bfloat16), 'seq', sc...]
    dot_general x11 -> x0, matrix products: 33 us -> none  [the longest x5 16.4 us: on_device(): jnp.dot(padded[k:k + length], conv_weight[k], preferred_element_type=jnp....]
    psum x1 -> x0, blocking collectives: 7.32 us -> none  [on_device(): lax.psum((jnp.sum(values, axis=1), jnp.sum(values * values, axis=1)), 'mp')]
    ppermute x2 -> x0, starting transfers between devices: 6.28 us -> none  [the longest x1 4.99 us: padded_2(): before = lax.ppermute(last, axis, up)]
  transfers between devices with their start and end apart: 6 -> 0, of which waited for: 5 -> 0; matrix products, arithmetic and copies ran while one was open for 22% -> 0% of each run, Pallas kernels for 0% -> 0%
where the time goes in v1:
time: 113 us; the launch traced here: 112 us
  Pallas kernels  104 us (92%)
  local copies, waits for them, and re-layouts  7.17 us (6%)
    pallas_call x1, Pallas kernels, on_device(): pl.pallas_call(kernel, name='block', out_shape=(jax.ShapeDtypeStruct((R,...  104 us
    unnamed x4, local copies, waits for them, and re-layouts  4.11 us

profile of v1, /device:TPU:1, one launch (start us, length us, event | category | flops | bytes accessed | tf_op | source)
XLA Modules:
  0.0 112.3 jit_solution(6020311608398194422)
XLA Ops:
  0.6 0.1 pad.8.clone
  0.7 1.2 %reshape.11.gain_hbm = f32[1,384]{1,0:T(1,128)} reshape(f32[384]{0:T(512)} %param.7) | data formatting | bytes 3072 | tf_op jit(solution)/shard_map/reshape | solution.py:416
  2.0 0.7 slice_bitcast_fusion.1
  2.7 1.0 fusion.3
  3.7 0.1 copy.9
  3.8 0.1 copy.10
  3.9 0.7 maximum_maximum_fusion.edge_hbm
  4.6 103.7 %block.1 = (bf16[512,640]{1,0:T(8,128)(2,1)}, f32[5,80,384]{2,1,0:T(8,128)}) custom-call(bf16[320,1024]{1,0:T(8,128)(2,1)} %bitcast.12, bf16[16,384]{1,0:T(8,128)(2,1)} %maximum_maximum_fusion.edge_hbm, bf16[5,1280,384]{2,1,0:T(8,128)(2,1)} %w_hbm.1, f32[1,384]{1,0:T(1,128)} %reshape.11.gain_hbm, bf16[1536,640]{1,0:T(8,128)(2,1)} %qw_hbm.1, ...), custom_call_target="tpu_custom_call" | custom-call | tf_op jit(solution)/shard_map/block/pallas_call | solution.py:399
  108.3 2.0 %copy.13 = bf16[1,512,640]{2,1,0:T(8,128)(2,1)} copy(bf16[1,512,640]{2,1,0:T(8,128)(2,1)} %bitcast.13) | data formatting | bytes 1310720
  110.3 1.9 %copy.14 = f32[80,5,384]{2,0,1:T(8,128)} copy(f32[80,5,384]{2,0,1:T(8,128)} %bitcast.14) | data formatting | bytes 1228800
  (2 shorter events, 0.0 us)

commit v2 on v1

v2 whole, which is shorter than its diff:
```python
import jax
import jax.numpy as jnp
from jax import lax
from jax.experimental import pallas as pl
from jax.experimental.pallas import tpu as pltpu
from jax.sharding import PartitionSpec as P

MESH = pl.DeviceIdType.MESH
BF16, F32 = jnp.bfloat16, jnp.float32
KW = 5
T = 1024
R = 512
CB = 320
O = 384
OT = O // 128
C = 4 * CB
N = KW * O
Q = 640
TB = 256
NB = T // TB
XB = 320
ZB = 80
COLS = (9 * 128, 6 * 128)
PIECE = (5 * 128, 3 * 128)
Y0 = 8

OWN_R, OWN_L, FWD_R, FWD_L = 0, 4, 8, 12
EDGE_UP, EDGE_DOWN, GRAD_UP, GRAD_DOWN, RIM, GAIN = 16, 17, 18, 19, 19, 22
ENC_R, ENC_L, EFWD_R, EFWD_L = 26, 28, 30, 31
SWAP = 32
X1R, X1L, X2R, X2L = 36, 37, 38, 40
ZUP, ZDN = 42, 46
DUP, DDN, DSW = 50, 51, 52
COPIES = 54


def kernel(
    xt_hbm, w_hbm, gain_hbm, qw_hbm, eg_hbm, qkv_hbm, cg_hbm,
    xt, ends, edge, rim, egrim, wcat, gain, qw, eg, xrow, yb, pgb, pgcat, enc, norm, qout,
    psend, precv, gown, x1l, x1r, x2l, x2r, zb, zru, zrd, zs, u1l, u1r, u2l, u2r, fin, cgo,
    lsem, ssem, rsem,
):
    seq, mp, dp = lax.axis_index("seq"), lax.axis_index("mp"), lax.axis_index("dp")
    x, zl = seq // 4, seq % 4
    zh, core = dp // 2, dp % 2
    z = zh * 4 + zl

    def at(s=None, m=None, d=None):
        return {"seq": seq if s is None else s, "mp": mp if m is None else m, "dp": dp if d is None else d}

    def z_at(zn):
        return at(s=x * 4 + zn % 4, d=(zn // 4) * 2 + core)

    y_right, y_left = at(m=(mp + 1) % 4), at(m=(mp + 3) % 4)
    s_up, s_down = at(s=(seq + 1) % 16), at(s=(seq + 15) % 16)
    x_right, x_left = at(s=(seq + 4) % 16), at(s=(seq + 12) % 16)
    z_up, z_down = z_at((z + 1) % 8), z_at((z + 7) % 8)
    partner = at(d=zh * 2 + 1 - core)
    z_up2, z_down2 = z_at((z + 2) % 8), z_at((z + 6) % 8)

    local = []

    def load(src, dst):
        copy = pltpu.make_async_copy(src, dst, lsem.at[len(local)])
        copy.start()
        local.append(copy)
        return copy

    own_rows = pl.ds(pl.multiple_of(mp * CB, CB), CB)
    end_loads = [load(xt_hbm.at[:, pl.ds(e * (T - 128), 128)], ends.at[e, pl.ds(0, CB)]) for e in (0, 1)]
    own_x = load(xt_hbm, xt.at[own_rows])
    loads = [load(w_hbm.at[k], wcat.at[:, pl.ds(k * O, O)]) for k in range(KW)]
    eg_load = load(eg_hbm, eg)
    gain_load = load(gain_hbm, gain.at[mp])
    qw_load = load(qw_hbm, qw)

    barrier = pltpu.get_barrier_semaphore()
    peers = [y_right, y_left, at(m=(mp + 2) % 4), s_up, s_down, x_right, x_left, z_up, z_down, z_up2, z_down2, partner]
    for peer in peers:
        pl.semaphore_signal(barrier, inc=1, device_id=peer, device_id_type=MESH)
    pl.semaphore_wait(barrier, len(peers))

    sent = []

    def remote(src, dst, i, peer):
        return pltpu.make_async_remote_copy(
            src_ref=src, dst_ref=dst, send_sem=ssem.at[i], recv_sem=rsem.at[i], device_id=peer, device_id_type=MESH
        )

    def send(src, dst, i, peer):
        copy = remote(src, dst, i, peer)
        copy.start()
        sent.append(copy)

    def arrived(dst, i):
        remote(dst, dst, i, y_right).wait_recv()

    def block(owner, half, tb):
        first = owner * CB + (0 if half is None else half * (CB // 2))
        size = CB if half is None else CB // 2
        return xt.at[pl.ds(pl.multiple_of(first, CB // 2), size), pl.ds(tb * TB, TB)]

    m_left, m_right, m_far = (mp + 3) % 4, (mp + 1) % 4, (mp + 2) % 4

    def send_own(tb):
        src = xt_hbm.at[:, pl.ds(tb * TB, TB)]
        send(src, block(mp, None, tb), OWN_R + tb, y_right)
        send(src, block(mp, None, tb), OWN_L + tb, y_left)

    def forward(tb):
        arrived(block(m_left, None, tb), OWN_R + tb)
        send(block(m_left, 0, tb), block(m_left, 0, tb), FWD_R + tb, y_right)
        arrived(block(m_right, None, tb), OWN_L + tb)
        send(block(m_right, 1, tb), block(m_right, 1, tb), FWD_L + tb, y_left)

    def complete(tb):
        arrived(block(m_far, 0, tb), FWD_R + tb)
        arrived(block(m_far, 1, tb), FWD_L + tb)

    send_own(0)
    send_own(1)
    for d in (1, 2, 3):
        send(gain_hbm, gain.at[mp], GAIN + d, at(m=(mp + d) % 4))
    send(eg_hbm.at[pl.ds(R - 16, 16)], egrim.at[0], GRAD_UP, s_up)
    send(eg_hbm.at[pl.ds(0, 16)], egrim.at[1], GRAD_DOWN, s_down)
    for copy in end_loads:
        copy.wait()
    for e in (0, 1):
        ends[e, CB:, :] = jnp.zeros((O - CB, 128), BF16)
        edge[e] = ends[e].T[112 * e : 112 * e + 16, :]
    send(edge.at[1], rim.at[mp, pl.ds(0, 16)], EDGE_UP, s_up)
    send(edge.at[0], rim.at[mp, pl.ds(16, 16)], EDGE_DOWN, s_down)
    own_x.wait()

    def tap_products(tb):
        xrow[...] = xt[:, tb * TB : (tb + 1) * TB].T

        def tile(n, carry):
            cols = pl.ds(pl.multiple_of(n * 256, 256), 256)
            y = jnp.dot(xrow[...], wcat[:, cols], preferred_element_type=F32)
            yb[2 * n, pl.ds(Y0 + tb * TB, TB), :] = y[:, :128]
            yb[2 * n + 1, pl.ds(Y0 + tb * TB, TB), :] = y[:, 128:]
            return carry

        lax.fori_loop(0, N // 256, tile, 0)
        y = jnp.dot(xrow[...], wcat[:, N - 128 :], preferred_element_type=F32)
        yb[N // 128 - 1, pl.ds(Y0 + tb * TB, TB), :] = y

    def rim_products():
        for d in (1, 2, 3):
            owner = (mp + 4 - d) % 4
            arrived(rim.at[owner], RIM + d)
        before = jnp.where(seq > 0, 1.0, 0.0).astype(F32)
        after = jnp.where(seq < 15, 1.0, 0.0).astype(F32)

        def tile(n, carry):
            cols = pl.ds(pl.multiple_of(n * 128, 128), 128)
            y = jnp.zeros((32, 128), F32)
            for m in range(4):
                y += jnp.dot(rim[m][:, :CB], wcat[m * CB : (m + 1) * CB, cols], preferred_element_type=F32)
            yb[n, pl.ds(0, 8), :] = y[8:16] * before
            yb[n, pl.ds(Y0 + T, 8), :] = y[16:24] * after
            return carry

        lax.fori_loop(0, N // 128, tile, 0)

    def gelu(v):
        v2 = v * v
        th = jnp.tanh(v * (0.7978845608 + (0.7978845608 * 0.044715) * v2))
        half = 0.5 + 0.5 * th
        slope = half + 0.5 * v * (1.0 - th * th) * (0.7978845608 + (0.7978845608 * 0.134145) * v2)
        return v * half, slope

    def pre(o, row, rows, stride):
        taps = [yb[k * OT + o, pl.ds(row + k - 2, rows, stride=stride), :] for k in range(KW)]
        return taps[0] + taps[1] + taps[2] + taps[3] + taps[4]

    STEP = 32

    def activations(first, count):
        def rows_of(i, carry):
            j = pl.multiple_of(first + i * STEP, STEP)
            for o in range(OT):
                lanes = pl.ds(o * 128, 128)
                act_e, slope_e = gelu(pre(o, Y0 + 2 * j, STEP, 2))
                act_o, slope_o = gelu(pre(o, Y0 + 2 * j + 1, STEP, 2))
                g = 0.5 * eg[pl.ds(j, STEP), lanes].astype(F32)
                enc[mp, pl.ds(j, STEP), lanes] = (0.5 * (act_e + act_o)).astype(BF16)
                pgb[o, pl.ds(Y0 + 2 * j, STEP, stride=2), :] = slope_e * g
                pgb[o, pl.ds(Y0 + 2 * j + 1, STEP, stride=2), :] = slope_o * g
            return carry

        lax.fori_loop(0, count // STEP, rows_of, 0)

    def rim_gradients():
        before = jnp.where(seq > 0, 0.5, 0.0).astype(F32)
        after = jnp.where(seq < 15, 0.5, 0.0).astype(F32)
        last, first = egrim[0, 8:16, :].astype(F32), egrim[1, 0:8, :].astype(F32)
        for o in range(OT):
            lanes = slice(o * 128, (o + 1) * 128)
            for row, g in ((Y0 - 2, last[7:8, lanes] * before), (Y0 + T, first[0:1, lanes] * after)):
                for r in (row, row + 1):
                    slope = gelu(pre(o, r, 1, 1))[1]
                    pgb[o, pl.ds(r, 1), :] = slope * g

    PSTEP = 64

    def gradient_columns():
        def rows_of(i, carry):
            s = pl.multiple_of(i * PSTEP, PSTEP)
            for k in range(KW):
                for o in range(OT):
                    pgcat[pl.ds(s, PSTEP), (k * OT + o) * 128 : (k * OT + o + 1) * 128] = pgb[
                        o, pl.ds(Y0 + s + 2 - k, PSTEP), :
                    ].astype(BF16)
            return carry

        lax.fori_loop(0, T // PSTEP, rows_of, 0)

    for copy in loads:
        copy.wait()
    forward(0)
    send_own(2)
    arrived(rim.at[mp, pl.ds(0, 16)], EDGE_UP)
    arrived(rim.at[mp, pl.ds(16, 16)], EDGE_DOWN)
    for d in (1, 2, 3):
        send(rim.at[mp], rim.at[mp], RIM + d, at(m=(mp + d) % 4))
    complete(0)
    tap_products(0)
    forward(1)
    send_own(3)
    rim_products()
    eg_load.wait()
    complete(1)
    tap_products(1)
    activations(0, 224)
    forward(2)
    forward(3)
    complete(2)
    tap_products(2)
    activations(224, 128)
    complete(3)
    tap_products(3)
    activations(352, 160)
    arrived(egrim.at[0], GRAD_UP)
    arrived(egrim.at[1], GRAD_DOWN)
    rim_gradients()

    def half_rows(owner, e):
        return enc.at[owner, pl.ds(e * (R // 2), R // 2)]

    send(half_rows(mp, 0), half_rows(mp, 0), ENC_R, y_right)
    send(half_rows(mp, 1), half_rows(mp, 1), ENC_L + 1, y_left)
    send(half_rows(mp, 1), half_rows(mp, 1), ENC_R + 1, y_right)
    send(half_rows(mp, 0), half_rows(mp, 0), ENC_L, y_left)
    gradient_columns()

    def rows_of_x(xb):
        return xt[pl.ds(pl.multiple_of(xb * XB, XB), XB), :]

    def rows_of_z(g):
        return jnp.concatenate(
            [xt[pl.ds(pl.multiple_of(xb * XB + g * ZB, ZB), ZB), :] for xb in range(4)], axis=0
        )

    def products(left, owner, write):
        first, width = owner * COLS[0], COLS[owner]

        def tile(n, carry):
            lane = pl.multiple_of(n * 256, 256)
            write(lane, 256, jnp.dot(left, pgcat[:, pl.ds(first + lane, 256)], preferred_element_type=F32))
            return carry

        lax.fori_loop(0, width // 256, tile, 0)
        if width % 256:
            lane = width // 256 * 256
            write(lane, 128, jnp.dot(left, pgcat[:, pl.ds(first + lane, 128)], preferred_element_type=F32))

    def theirs(other, step, b):
        def write(lane, width, value):
            psend[b, :, pl.ds(lane, width)] = value.astype(BF16)

        products((rows_of_z if other else rows_of_x)(b), other, write)
        cols = pl.ds(0, COLS[other])
        send(psend.at[b, :, cols], precv.at[b, :, cols], SWAP + step, partner)

    def ours(me, step, b):
        arrived(precv.at[b, :, pl.ds(0, COLS[me])], SWAP + step)

        def write(lane, width, value):
            cols = pl.ds(lane, width)
            gown[b, :, cols] = (value + precv[b, :, cols].astype(F32)).astype(BF16)

        products((rows_of_z if me else rows_of_x)(b), me, write)

    def add(dst, src):
        for r in range(0, dst.shape[0], 16):
            rows = pl.ds(r, 16)
            dst[rows, :] = (dst[rows, :].astype(F32) + src[rows, :].astype(F32)).astype(BF16)

    def add3(dst, a, b, c):
        for r in range(0, dst.shape[0], 16):
            rows = pl.ds(r, 16)
            dst[rows, :] = (a[rows, :].astype(F32) + b[rows, :].astype(F32) + c[rows, :].astype(F32)).astype(BF16)

    def forward_encoded():
        arrived(half_rows(m_left, 0), ENC_R)
        send(half_rows(m_left, 0), half_rows(m_left, 0), EFWD_R, y_right)
        arrived(half_rows(m_right, 1), ENC_L + 1)
        send(half_rows(m_right, 1), half_rows(m_right, 1), EFWD_L, y_left)

    def encoded_complete():
        arrived(half_rows(m_left, 1), ENC_R + 1)
        arrived(half_rows(m_right, 0), ENC_L)
        arrived(half_rows(m_far, 0), EFWD_R)
        arrived(half_rows(m_far, 1), EFWD_L)
        gain_load.wait()
        for d in (1, 2, 3):
            arrived(gain.at[(mp + 4 - d) % 4], GAIN + d)
        qw_load.wait()

    def heads(part):
        def normalize(i, carry):
            rows = pl.ds(pl.multiple_of(part * 128 + i * 32, 32), 32)
            values = [enc[m, rows, :].astype(F32) for m in range(4)]
            total = jnp.sum(values[0] + values[1] + values[2] + values[3], axis=1, keepdims=True)
            square = jnp.sum(sum(v * v for v in values), axis=1, keepdims=True)
            mean = total / (4 * O)
            scale = lax.rsqrt(square / (4 * O) - mean * mean + 1e-05)
            for m in range(4):
                norm[rows, m * O : (m + 1) * O] = ((values[m] - mean) * scale * gain[m]).astype(BF16)
            return carry

        lax.fori_loop(0, 4, normalize, 0)
        rows = pl.ds(part * 128, 128)
        qout[rows, :] = jnp.dot(norm[rows, :], qw[...], preferred_element_type=F32).astype(BF16)

    top, bottom = pl.ds(0, XB // 2), pl.ds(XB // 2, XB // 2)
    xf, xr, xl = (x + 2) % 4, (x + 1) % 4, (x + 3) % 4
    gf, gr, gl = (zl + 2) % 4, (zl + 1) % 4, (zl + 3) % 4

    def share(me, mine):
        cols = pl.ds(0, PIECE[me])
        send(mine, fin.at[me, zh, :, cols], DUP, z_up2)
        send(mine, fin.at[me, zh, :, cols], DDN, z_down2)
        lower, upper = (z + 6) % 8 // 4, (z + 2) % 8 // 4
        arrived(fin.at[me, lower, :, cols], DUP)
        send(fin.at[me, lower, :, cols], fin.at[me, lower, :, cols], DSW, partner)
        arrived(fin.at[me, upper, :, cols], DDN)
        send(fin.at[me, upper, :, cols], fin.at[me, upper, :, cols], DSW + 1, partner)
        cols = pl.ds(0, PIECE[1 - me])
        arrived(fin.at[1 - me, lower, :, cols], DSW)
        arrived(fin.at[1 - me, upper, :, cols], DSW + 1)

    shared = len(sent)

    @pl.when(core == 0)
    def _():
        theirs(1, 0, gf)
        theirs(1, 1, gr)
        theirs(1, 2, gl)
        ours(0, 0, xf)
        send(gown.at[xf, top], x1l, X1R, x_right)
        send(gown.at[xf, bottom], x1r, X1L, x_left)
        theirs(1, 3, zl)
        ours(0, 1, xr)
        send(gown.at[xr, bottom], x2l.at[bottom], X2R + 1, x_right)
        forward_encoded()
        ours(0, 2, xl)
        send(gown.at[xl, top], x2r.at[top], X2L, x_left)
        arrived(x1l, X1R)
        add(gown.at[xr, top], x1l)
        send(gown.at[xr, top], x2l.at[top], X2R, x_right)
        arrived(x1r, X1L)
        add(gown.at[xl, bottom], x1r)
        send(gown.at[xl, bottom], x2r.at[bottom], X2L + 1, x_left)
        ours(0, 3, x)
        encoded_complete()
        heads(0)
        for half, rows in ((0, top), (1, bottom)):
            arrived(x2l.at[rows], X2R + half)
            arrived(x2r.at[rows], X2L + half)
        for g in range(4):
            for h in range(2):
                rows, cols = pl.ds(g * ZB, ZB), pl.ds(h * 512, 640)
                add3(zb.at[g, h], gown.at[x, rows, cols], x2l.at[rows, cols], x2r.at[rows, cols])

        def piece(zo):
            return zb.at[(zo + 2) % 4, zo // 4]

        up, down = pl.ds(0, 384), pl.ds(384, 256)
        far = piece((z + 4) % 8)
        ru = [zru.at[s, pl.ds(0, ZB)] for s in range(4)]
        rd = [zrd.at[s, pl.ds(0, ZB)] for s in range(4)]
        send(far.at[:, up], ru[0].at[:, up], ZUP, z_up)
        send(far.at[:, down], rd[0].at[:, down], ZDN, z_down)
        for step in (1, 2, 3):
            heads(step)
            higher, lower = piece((z + 4 - step) % 8), piece((z + 4 + step) % 8)
            cu, cd = (up, down) if step == 1 else (pl.ds(0, 640),) * 2
            arrived(ru[step - 1].at[:, cu], ZUP + step - 1)
            add(higher.at[:, cu], ru[step - 1].at[:, cu])
            send(higher, ru[step], ZUP + step, z_up)
            arrived(rd[step - 1].at[:, cd], ZDN + step - 1)
            add(lower.at[:, cd], rd[step - 1].at[:, cd])
            send(lower, rd[step], ZDN + step, z_down)
        load(qout, qkv_hbm)
        arrived(ru[3], ZUP + 3)
        arrived(rd[3], ZDN + 3)
        mine = piece(z)
        add3(mine, mine, ru[3], rd[3])
        share(0, mine)
        for copy in sent:
            copy.wait_send()
        local[-1].wait()

    @pl.when(core == 1)
    def _():
        del sent[shared:]
        theirs(0, 0, xf)
        theirs(0, 1, xr)
        ours(1, 0, gf)

        def piece(zo):
            return gown.at[(zo + 2) % 4, :, pl.ds(pl.multiple_of(zo // 4 * PIECE[1], 128), PIECE[1])]

        ru = [zru.at[s, :, pl.ds(0, PIECE[1])] for s in range(4)]
        rd = [zrd.at[s, :, pl.ds(0, PIECE[1])] for s in range(4)]

        def up(step):
            dst = piece((z + 4 - step) % 8)
            rows = top if step == 1 else pl.ds(0, XB)
            arrived(ru[step - 1].at[rows], ZUP + step - 1)
            add(dst.at[rows], ru[step - 1].at[rows])
            send(dst, ru[step], ZUP + step, z_up)

        def down(step):
            dst = piece((z + 4 + step) % 8)
            rows = bottom if step == 1 else pl.ds(0, XB)
            arrived(rd[step - 1].at[rows], ZDN + step - 1)
            add(dst.at[rows], rd[step - 1].at[rows])
            send(dst, rd[step], ZDN + step, z_down)

        far = piece((z + 4) % 8)
        send(far.at[top], ru[0].at[top], ZUP, z_up)
        send(far.at[bottom], rd[0].at[bottom], ZDN, z_down)
        theirs(0, 2, xl)
        ours(1, 1, gr)
        up(1)
        ours(1, 2, gl)
        down(1)
        theirs(0, 3, x)
        forward_encoded()
        ours(1, 3, zl)
        up(2)
        down(2)
        up(3)
        down(3)
        encoded_complete()
        heads(0)
        heads(1)
        arrived(ru[3], ZUP + 3)
        arrived(rd[3], ZDN + 3)
        add3(zs, piece(z), ru[3], rd[3])

        def rows_at(xb, first, rows):
            return zs.at[pl.ds(pl.multiple_of(xb * ZB + first, 16), rows)]

        send(rows_at(xf, 0, 48), u1l, X1R, x_right)
        send(rows_at(xf, 48, 32), u1r, X1L, x_left)
        heads(2)
        arrived(u1l, X1R)
        add(rows_at(xr, 0, 48), u1l)
        send(rows_at(xr, 0, ZB), u2l, X2R, x_right)
        arrived(u1r, X1L)
        add(rows_at(xl, 48, 32), u1r)
        send(rows_at(xl, 0, ZB), u2r, X2L, x_left)
        heads(3)
        load(qout, qkv_hbm)
        arrived(u2l, X2R)
        arrived(u2r, X2L)
        mine = rows_at(x, 0, ZB)
        add3(mine, mine, u2l, u2r)
        share(1, mine)
        for copy in sent:
            copy.wait_send()
        local[-1].wait()

    for i in range(N // 128):
        if i < 9:
            src = fin.at[0, i // 5, :, pl.ds((i - i // 5 * 4) * 128, 128)]
        else:
            src = fin.at[1, (i - 9) // 3, :, pl.ds((i - 9) % 3 * 128, 128)]
        cgo[i // OT, :, pl.ds((i % OT) * 128, 128)] = src[...]
    load(cgo, cg_hbm).wait()


def finish(qkv_in, grad_in, qkv_out, grad_out, qkv, grad, wide, sem):
    first = pltpu.make_async_copy(grad_in, grad, sem.at[0])
    second = pltpu.make_async_copy(qkv_in, qkv, sem.at[1])
    first.start()
    second.start()
    first.wait()
    wide[...] = grad[...].astype(F32)
    third = pltpu.make_async_copy(wide, grad_out, sem.at[2])
    third.start()
    second.wait()
    fourth = pltpu.make_async_copy(qkv, qkv_out, sem.at[3])
    fourth.start()
    third.wait()
    fourth.wait()


def on_device(block_input, conv_weight, norm_gain, qkv_weight, encoder_grad):
    xin, eg = block_input[0], encoder_grad[0]
    any_ = pl.BlockSpec(memory_space=pl.ANY)
    v = pltpu.VMEM
    qkv, grad = pl.pallas_call(
        kernel,
        name="block",
        out_shape=(jax.ShapeDtypeStruct((R, Q), BF16), jax.ShapeDtypeStruct((KW, ZB, O), BF16)),
        in_specs=[any_] * 5,
        out_specs=(any_, any_),
        scratch_shapes=[
            v((C, T), BF16), v((2, O, 128), BF16), v((2, 16, O), BF16), v((4, 32, O), BF16), v((2, 16, O), BF16),
            v((C, N), BF16), v((4, O), F32), v((4 * O, Q), BF16), v((R, O), BF16),
            v((TB, C), BF16), v((N // 128, T + 16, 128), F32), v((OT, T + 16, 128), F32), v((T, N), BF16),
            v((4, R, O), BF16), v((R, 4 * O), BF16), v((R, Q), BF16),
            v((4, XB, COLS[0]), BF16), v((4, XB, COLS[0]), BF16), v((4, XB, COLS[0]), BF16),
            v((XB // 2, COLS[0]), BF16), v((XB // 2, COLS[0]), BF16), v((XB, COLS[0]), BF16), v((XB, COLS[0]), BF16),
            v((4, 2, ZB, PIECE[0]), BF16), v((4, XB, PIECE[0]), BF16), v((4, XB, PIECE[0]), BF16), v((XB, PIECE[1]), BF16),
            v((48, PIECE[1]), BF16), v((32, PIECE[1]), BF16), v((ZB, PIECE[1]), BF16), v((ZB, PIECE[1]), BF16),
            v((2, 2, ZB, PIECE[0]), BF16), v((KW, ZB, O), BF16),
            pltpu.SemaphoreType.DMA((16,)), pltpu.SemaphoreType.DMA((COPIES,)), pltpu.SemaphoreType.DMA((COPIES,)),
        ],
        compiler_params=pltpu.CompilerParams(collective_id=0, has_side_effects=True, vmem_limit_bytes=58 * 2**20),
    )(xin.T, conv_weight, norm_gain, qkv_weight, eg)
    qkv, grad = pl.pallas_call(
        finish,
        name="finish",
        out_shape=(jax.ShapeDtypeStruct((R, Q), BF16), jax.ShapeDtypeStruct((KW, ZB, O), F32)),
        in_specs=[any_] * 2,
        out_specs=(any_, any_),
        scratch_shapes=[v((R, Q), BF16), v((KW, ZB, O), BF16), v((KW, ZB, O), F32), pltpu.SemaphoreType.DMA((4,))],
    )(qkv, grad)
    return qkv[None], grad.transpose(1, 0, 2)


def solution(mesh):
    return jax.shard_map(
        on_device,
        mesh=mesh,
        in_specs=(
            P("dp", "seq", "mp"),
            P(None, None, "mp"),
            P("mp"),
            P(None, "mp"),
            P("dp", "seq", "mp"),
        ),
        out_specs=(P("dp", "seq", "mp"), P("seq", None, "mp")),
        check_vma=False,
    )
```

time: 113 us -> 91.8 us (0.81)
  Pallas kernels: 104 us -> 90.9 us
  local copies, waits for them, and re-layouts: 7.17 us -> 0 us
    pallas_call x1, Pallas kernels: 104 us -> 88.8 us  [on_device(): pl.pallas_call(kernel, name='block', out_shape=(jax.ShapeDtypeStruct((R,...]
    unnamed x4 -> x0, local copies, waits for them, and re-layouts: 4.11 us -> none
    pallas_call x0 -> x1, Pallas kernels: none -> 2.08 us  [on_device(): pl.pallas_call(finish, name='finish', out_shape=(jax.ShapeDtypeStruct((R,...]
    slice x2 -> x0, local copies, waits for them, and re-layouts: 1.73 us -> none  [the longest x1 1.02 us: on_device(): xin[:4]]
    reshape x1 -> x0, local copies, waits for them, and re-layouts: 1.24 us -> none  [on_device(): norm_gain.reshape(1, O)]
where the time goes in v2:
time: 91.8 us; the launch traced here: 91.7 us
  Pallas kernels  90.9 us (99%)
    pallas_call x1, Pallas kernels, on_device(): pl.pallas_call(kernel, name='block', out_shape=(jax.ShapeDtypeStruct((R,...  88.8 us
    pallas_call x1, Pallas kernels, on_device(): pl.pallas_call(finish, name='finish', out_shape=(jax.ShapeDtypeStruct((R,...  2.08 us

profile of v2, /device:TPU:1, one launch (start us, length us, event | category | flops | bytes accessed | tf_op | source)
XLA Modules:
  0.0 91.7 jit_solution(14069265748221291237)
XLA Ops:
  0.6 88.8 %block.1 = (bf16[512,640]{1,0:T(8,128)(2,1)}, bf16[5,80,384]{2,1,0:T(8,128)(2,1)}) custom-call(bf16[320,1024]{1,0:T(8,128)(2,1)} %bitcast.6, bf16[5,1280,384]{2,1,0:T(8,128)(2,1)} %w_hbm.1, f32[384]{0:T(512)} %gain_hbm.1, bf16[1536,640]{1,0:T(8,128)(2,1)} %qw_hbm.1, bf16[512,384]{1,0:T(8,128)(2,1)} %bitcast.7), custom_call_target="tpu_custom_call" | custom-call | tf_op jit(solution)/shard_map/block/pallas_call | solution.py:518
  89.4 2.1 %finish.1 = (bf16[512,640]{1,0:T(8,128)(2,1)}, f32[5,80,384]{2,1,0:T(8,128)}) custom-call(bf16[512,640]{1,0:T(8,128)(2,1)} %get-tuple-element.6.qkv_in, bf16[5,80,384]{2,1,0:T(8,128)(2,1)} %get-tuple-element.7.grad_in), custom_call_target="tpu_custom_call" | custom-call | tf_op jit(solution)/shard_map/finish/pallas_call | solution.py:538

commit v3 on v2

--- a/solution.py
+++ b/solution.py
@@ -16,28 +16,28 @@
 C = 4 * CB
 N = KW * O
 Q = 640
-TB = 256
-NB = T // TB
+TB = 128
+TC = 256
 XB = 320
 ZB = 80
 COLS = (9 * 128, 6 * 128)
-PIECE = (5 * 128, 3 * 128)
+PIECE = 3 * 128
 Y0 = 8
 
-OWN_R, OWN_L, FWD_R, FWD_L = 0, 4, 8, 12
-EDGE_UP, EDGE_DOWN, GRAD_UP, GRAD_DOWN, RIM, GAIN = 16, 17, 18, 19, 19, 22
-ENC_R, ENC_L, EFWD_R, EFWD_L = 26, 28, 30, 31
-SWAP = 32
-X1R, X1L, X2R, X2L = 36, 37, 38, 40
-ZUP, ZDN = 42, 46
-DUP, DDN, DSW = 50, 51, 52
-COPIES = 54
+OWN_R, OWN_L, FWD_R, FWD_L = 0, 8, 16, 24
+EDGE_UP, EDGE_DOWN, GRAD_UP, GRAD_DOWN, RIM, GAIN = 32, 33, 34, 35, 35, 38
+ENC_R, ENC_L, EFWD_R, EFWD_L = 42, 44, 46, 47
+SWAP = 48
+X1R, X1L, X2R, X2L = 52, 53, 54, 56
+ZUA, ZUB, ZDA, ZDB = 58, 62, 66, 70
+DUP, DDN, DSW = 74, 75, 76
+COPIES = 78
 
 
 def kernel(
     xt_hbm, w_hbm, gain_hbm, qw_hbm, eg_hbm, qkv_hbm, cg_hbm,
     xt, ends, edge, rim, egrim, wcat, gain, qw, eg, xrow, yb, pgb, pgcat, enc, norm, qout,
-    psend, precv, gown, x1l, x1r, x2l, x2r, zb, zru, zrd, zs, u1l, u1r, u2l, u2r, fin, cgo,
+    psend, precv, gown, x1l, x1r, x2l, x2r, zb, zr, zs, zr1, zs1, u1l, u1r, u2l, u2r, fin0, fin1, cgo,
     lsem, ssem, rsem,
 ):
     seq, mp, dp = lax.axis_index("seq"), lax.axis_index("mp"), lax.axis_index("dp")
@@ -132,19 +132,23 @@
     send(edge.at[0], rim.at[mp, pl.ds(16, 16)], EDGE_DOWN, s_down)
     own_x.wait()
 
-    def tap_products(tb):
-        xrow[...] = xt[:, tb * TB : (tb + 1) * TB].T
+    def tap_products(g, half):
+        if half == 0:
+            xrow[...] = xt[:, g * TC : (g + 1) * TC].T
 
         def tile(n, carry):
             cols = pl.ds(pl.multiple_of(n * 256, 256), 256)
             y = jnp.dot(xrow[...], wcat[:, cols], preferred_element_type=F32)
-            yb[2 * n, pl.ds(Y0 + tb * TB, TB), :] = y[:, :128]
-            yb[2 * n + 1, pl.ds(Y0 + tb * TB, TB), :] = y[:, 128:]
+            yb[2 * n, pl.ds(Y0 + g * TC, TC), :] = y[:, :128]
+            yb[2 * n + 1, pl.ds(Y0 + g * TC, TC), :] = y[:, 128:]
             return carry
 
-        lax.fori_loop(0, N // 256, tile, 0)
-        y = jnp.dot(xrow[...], wcat[:, N - 128 :], preferred_element_type=F32)
-        yb[N // 128 - 1, pl.ds(Y0 + tb * TB, TB), :] = y
+        if half == 0:
+            lax.fori_loop(0, 4, tile, 0)
+        else:
+            lax.fori_loop(4, N // 256, tile, 0)
+            y = jnp.dot(xrow[...], wcat[:, N - 128 :], preferred_element_type=F32)
+            yb[N // 128 - 1, pl.ds(Y0 + g * TC, TC), :] = y
 
     def rim_products():
         for d in (1, 2, 3):
@@ -192,22 +196,22 @@
 
         lax.fori_loop(0, count // STEP, rows_of, 0)
 
-    def rim_gradients():
+    def rim_gradients(side):
         before = jnp.where(seq > 0, 0.5, 0.0).astype(F32)
         after = jnp.where(seq < 15, 0.5, 0.0).astype(F32)
         last, first = egrim[0, 8:16, :].astype(F32), egrim[1, 0:8, :].astype(F32)
         for o in range(OT):
             lanes = slice(o * 128, (o + 1) * 128)
-            for row, g in ((Y0 - 2, last[7:8, lanes] * before), (Y0 + T, first[0:1, lanes] * after)):
-                for r in (row, row + 1):
-                    slope = gelu(pre(o, r, 1, 1))[1]
-                    pgb[o, pl.ds(r, 1), :] = slope * g
+            row, g = ((Y0 - 2, last[7:8, lanes] * before), (Y0 + T, first[0:1, lanes] * after))[side]
+            for r in (row, row + 1):
+                slope = gelu(pre(o, r, 1, 1))[1]
+                pgb[o, pl.ds(r, 1), :] = slope * g
 
     PSTEP = 64
 
-    def gradient_columns():
+    def gradient_columns(first, count):
         def rows_of(i, carry):
-            s = pl.multiple_of(i * PSTEP, PSTEP)
+            s = pl.multiple_of(first + i * PSTEP, PSTEP)
             for k in range(KW):
                 for o in range(OT):
                     pgcat[pl.ds(s, PSTEP), (k * OT + o) * 128 : (k * OT + o + 1) * 128] = pgb[
@@ -215,36 +219,53 @@
                     ].astype(BF16)
             return carry
 
-        lax.fori_loop(0, T // PSTEP, rows_of, 0)
-
-    for copy in loads:
-        copy.wait()
-    forward(0)
-    send_own(2)
+        lax.fori_loop(0, count // PSTEP, rows_of, 0)
+
+    def serve(i):
+        forward(i)
+        if i + 2 < T // TB:
+            send_own(i + 2)
+
+    def group(g):
+        complete(2 * g)
+        complete(2 * g + 1)
+
+    serve(0)
     arrived(rim.at[mp, pl.ds(0, 16)], EDGE_UP)
     arrived(rim.at[mp, pl.ds(16, 16)], EDGE_DOWN)
     for d in (1, 2, 3):
         send(rim.at[mp], rim.at[mp], RIM + d, at(m=(mp + d) % 4))
-    complete(0)
-    tap_products(0)
-    forward(1)
-    send_own(3)
+    serve(1)
+    for copy in loads:
+        copy.wait()
+    serve(2)
+    group(0)
+    tap_products(0, 0)
+    serve(3)
+    tap_products(0, 1)
     rim_products()
+    serve(4)
+    group(1)
+    tap_products(1, 0)
+    serve(5)
+    tap_products(1, 1)
     eg_load.wait()
-    complete(1)
-    tap_products(1)
     activations(0, 224)
-    forward(2)
-    forward(3)
-    complete(2)
-    tap_products(2)
-    activations(224, 128)
-    complete(3)
-    tap_products(3)
-    activations(352, 160)
     arrived(egrim.at[0], GRAD_UP)
     arrived(egrim.at[1], GRAD_DOWN)
-    rim_gradients()
+    rim_gradients(0)
+    serve(6)
+    gradient_columns(0, 384)
+    group(2)
+    tap_products(2, 0)
+    serve(7)
+    tap_products(2, 1)
+    activations(224, 128)
+    group(3)
+    tap_products(3, 0)
+    tap_products(3, 1)
+    activations(352, 160)
+    rim_gradients(1)
 
     def half_rows(owner, e):
         return enc.at[owner, pl.ds(e * (R // 2), R // 2)]
@@ -253,7 +274,7 @@
     send(half_rows(mp, 1), half_rows(mp, 1), ENC_L + 1, y_left)
     send(half_rows(mp, 1), half_rows(mp, 1), ENC_R + 1, y_right)
     send(half_rows(mp, 0), half_rows(mp, 0), ENC_L, y_left)
-    gradient_columns()
+    gradient_columns(384, 640)
 
     def rows_of_x(xb):
         return xt[pl.ds(pl.multiple_of(xb * XB, XB), XB), :]
@@ -297,6 +318,11 @@
         for r in range(0, dst.shape[0], 16):
             rows = pl.ds(r, 16)
             dst[rows, :] = (dst[rows, :].astype(F32) + src[rows, :].astype(F32)).astype(BF16)
+
+    def add_to(dst, a, b):
+        for r in range(0, dst.shape[0], 16):
+            rows = pl.ds(r, 16)
+            dst[rows, :] = (a[rows, :].astype(F32) + b[rows, :].astype(F32)).astype(BF16)
 
     def add3(dst, a, b, c):
         for r in range(0, dst.shape[0], 16):
@@ -339,18 +365,25 @@
     xf, xr, xl = (x + 2) % 4, (x + 1) % 4, (x + 3) % 4
     gf, gr, gl = (zl + 2) % 4, (zl + 1) % 4, (zl + 3) % 4
 
-    def share(me, mine):
-        cols = pl.ds(0, PIECE[me])
-        send(mine, fin.at[me, zh, :, cols], DUP, z_up2)
-        send(mine, fin.at[me, zh, :, cols], DDN, z_down2)
-        lower, upper = (z + 6) % 8 // 4, (z + 2) % 8 // 4
-        arrived(fin.at[me, lower, :, cols], DUP)
-        send(fin.at[me, lower, :, cols], fin.at[me, lower, :, cols], DSW, partner)
-        arrived(fin.at[me, upper, :, cols], DDN)
-        send(fin.at[me, upper, :, cols], fin.at[me, upper, :, cols], DSW + 1, partner)
-        cols = pl.ds(0, PIECE[1 - me])
-        arrived(fin.at[1 - me, lower, :, cols], DSW)
-        arrived(fin.at[1 - me, upper, :, cols], DSW + 1)
+    lower, upper = (z + 6) % 8 // 4, (z + 2) % 8 // 4
+
+    def z_chain(step, part, base, received, staged):
+        for sign, ids, peer in ((1, (ZUA, ZUB), z_up), (-1, (ZDA, ZDB), z_down)):
+            z_hop(sign, step, part, base, received, staged, ids[part] + step - 1, peer)
+
+    def z_hop(sign, step, part, base, received, staged, i, peer):
+        src = base(sign, step, part)
+        if step > 1 + part:
+            arrived(received(sign, step - 1, part), i - 1)
+            dst = staged(sign, step, part)
+            add_to(dst, src, received(sign, step - 1, part))
+            src = dst
+        send(src, received(sign, step, part), i, peer)
+
+    def z_last(received):
+        for sign, ids in ((1, (ZUA, ZUB)), (-1, (ZDA, ZDB))):
+            for part in (0, 1):
+                arrived(received(sign, 4, part), ids[part] + 3)
 
     shared = len(sent)
 
@@ -381,35 +414,42 @@
             arrived(x2l.at[rows], X2R + half)
             arrived(x2r.at[rows], X2L + half)
         for g in range(4):
-            for h in range(2):
-                rows, cols = pl.ds(g * ZB, ZB), pl.ds(h * 512, 640)
-                add3(zb.at[g, h], gown.at[x, rows, cols], x2l.at[rows, cols], x2r.at[rows, cols])
-
-        def piece(zo):
-            return zb.at[(zo + 2) % 4, zo // 4]
-
-        up, down = pl.ds(0, 384), pl.ds(384, 256)
-        far = piece((z + 4) % 8)
-        ru = [zru.at[s, pl.ds(0, ZB)] for s in range(4)]
-        rd = [zrd.at[s, pl.ds(0, ZB)] for s in range(4)]
-        send(far.at[:, up], ru[0].at[:, up], ZUP, z_up)
-        send(far.at[:, down], rd[0].at[:, down], ZDN, z_down)
-        for step in (1, 2, 3):
-            heads(step)
-            higher, lower = piece((z + 4 - step) % 8), piece((z + 4 + step) % 8)
-            cu, cd = (up, down) if step == 1 else (pl.ds(0, 640),) * 2
-            arrived(ru[step - 1].at[:, cu], ZUP + step - 1)
-            add(higher.at[:, cu], ru[step - 1].at[:, cu])
-            send(higher, ru[step], ZUP + step, z_up)
-            arrived(rd[step - 1].at[:, cd], ZDN + step - 1)
-            add(lower.at[:, cd], rd[step - 1].at[:, cd])
-            send(lower, rd[step], ZDN + step, z_down)
+            rows = pl.ds(g * ZB, ZB)
+            add3(zb.at[g], gown.at[x, rows], x2l.at[rows], x2r.at[rows])
+
+        spans = (pl.ds(0, 640), pl.ds(640, 512))
+
+        def cols(sign, part):
+            return spans[part if sign == 1 else 1 - part]
+
+        def way(sign):
+            return 0 if sign == 1 else 1
+
+        def base(sign, step, part):
+            return zb.at[(zl + 5 - step if sign == 1 else zl + 3 + step) % 4, :, cols(sign, part)]
+
+        def received(sign, step, part):
+            return zr.at[way(sign), step - 1, :, cols(sign, part)]
+
+        def staged(sign, step, part):
+            return zs.at[way(sign), step - 2, :, cols(sign, part)]
+
+        z_chain(1, 0, base, received, staged)
+        z_chain(2, 1, base, received, staged)
+        heads(1)
+        z_chain(2, 0, base, received, staged)
+        z_chain(3, 1, base, received, staged)
+        heads(2)
+        z_chain(3, 0, base, received, staged)
+        z_chain(4, 1, base, received, staged)
+        heads(3)
         load(qout, qkv_hbm)
-        arrived(ru[3], ZUP + 3)
-        arrived(rd[3], ZDN + 3)
-        mine = piece(z)
-        add3(mine, mine, ru[3], rd[3])
-        share(0, mine)
+        z_chain(4, 0, base, received, staged)
+        z_last(received)
+        add3(fin0, zb.at[zl], zr.at[0, 3], zr.at[1, 3])
+        send(fin0, fin0, DSW, partner)
+        arrived(fin1.at[lower], DSW)
+        arrived(fin1.at[upper], DSW + 1)
         for copy in sent:
             copy.wait_send()
         local[-1].wait()
@@ -422,75 +462,76 @@
         ours(1, 0, gf)
 
         def piece(zo):
-            return gown.at[(zo + 2) % 4, :, pl.ds(pl.multiple_of(zo // 4 * PIECE[1], 128), PIECE[1])]
-
-        ru = [zru.at[s, :, pl.ds(0, PIECE[1])] for s in range(4)]
-        rd = [zrd.at[s, :, pl.ds(0, PIECE[1])] for s in range(4)]
-
-        def up(step):
-            dst = piece((z + 4 - step) % 8)
-            rows = top if step == 1 else pl.ds(0, XB)
-            arrived(ru[step - 1].at[rows], ZUP + step - 1)
-            add(dst.at[rows], ru[step - 1].at[rows])
-            send(dst, ru[step], ZUP + step, z_up)
-
-        def down(step):
-            dst = piece((z + 4 + step) % 8)
-            rows = bottom if step == 1 else pl.ds(0, XB)
-            arrived(rd[step - 1].at[rows], ZDN + step - 1)
-            add(dst.at[rows], rd[step - 1].at[rows])
-            send(dst, rd[step], ZDN + step, z_down)
-
-        far = piece((z + 4) % 8)
-        send(far.at[top], ru[0].at[top], ZUP, z_up)
-        send(far.at[bottom], rd[0].at[bottom], ZDN, z_down)
+            return gown.at[(zo + 2) % 4, :, pl.ds(pl.multiple_of(zo // 4 * PIECE, 128), PIECE)]
+
+        def half(ref, sign, part):
+            return ref.at[top if (part == 0) == (sign == 1) else bottom]
+
+        def base(sign, step, part):
+            return half(piece((z + 5 - step if sign == 1 else z + 3 + step) % 8), sign, part)
+
+        def received(sign, step, part):
+            return half(zr1.at[0 if sign == 1 else 1, step - 1], sign, part)
+
+        def hop(sign, step, part):
+            i, peer = ((ZUA, ZUB)[part], z_up) if sign == 1 else ((ZDA, ZDB)[part], z_down)
+            z_hop(sign, step, part, base, received, base, i + step - 1, peer)
+
+        z_chain(1, 0, base, received, base)
         theirs(0, 2, xl)
         ours(1, 1, gr)
-        up(1)
+        hop(1, 2, 1)
+        hop(1, 2, 0)
         ours(1, 2, gl)
-        down(1)
+        hop(-1, 2, 1)
+        hop(-1, 2, 0)
         theirs(0, 3, x)
+        ours(1, 3, zl)
+        z_chain(3, 1, base, received, base)
+        z_chain(3, 0, base, received, base)
         forward_encoded()
-        ours(1, 3, zl)
-        up(2)
-        down(2)
-        up(3)
-        down(3)
+        z_chain(4, 1, base, received, base)
+        z_chain(4, 0, base, received, base)
         encoded_complete()
         heads(0)
-        heads(1)
-        arrived(ru[3], ZUP + 3)
-        arrived(rd[3], ZDN + 3)
-        add3(zs, piece(z), ru[3], rd[3])
+        z_last(received)
+        add3(zs1, piece(z), zr1.at[0, 3], zr1.at[1, 3])
 
         def rows_at(xb, first, rows):
-            return zs.at[pl.ds(pl.multiple_of(xb * ZB + first, 16), rows)]
+            return zs1.at[pl.ds(pl.multiple_of(xb * ZB + first, 16), rows)]
 
         send(rows_at(xf, 0, 48), u1l, X1R, x_right)
         send(rows_at(xf, 48, 32), u1r, X1L, x_left)
-        heads(2)
+        heads(1)
         arrived(u1l, X1R)
         add(rows_at(xr, 0, 48), u1l)
         send(rows_at(xr, 0, ZB), u2l, X2R, x_right)
         arrived(u1r, X1L)
         add(rows_at(xl, 48, 32), u1r)
         send(rows_at(xl, 0, ZB), u2r, X2L, x_left)
-        heads(3)
-        load(qout, qkv_hbm)
+        heads(2)
         arrived(u2l, X2R)
         arrived(u2r, X2L)
         mine = rows_at(x, 0, ZB)
         add3(mine, mine, u2l, u2r)
-        share(1, mine)
+        send(mine, fin1.at[zh], DUP, z_up2)
+        send(mine, fin1.at[zh], DDN, z_down2)
+        heads(3)
+        load(qout, qkv_hbm)
+        arrived(fin1.at[lower], DUP)
+        send(fin1.at[lower], fin1.at[lower], DSW, partner)
+        arrived(fin1.at[upper], DDN)
+        send(fin1.at[upper], fin1.at[upper], DSW + 1, partner)
+        arrived(fin0, DSW)
         for copy in sent:
             copy.wait_send()
         local[-1].wait()
 
     for i in range(N // 128):
         if i < 9:
-            src = fin.at[0, i // 5, :, pl.ds((i - i // 5 * 4) * 128, 128)]
+            src = fin0.at[:, pl.ds(i * 128, 128)]
         else:
-            src = fin.at[1, (i - 9) // 3, :, pl.ds((i - 9) % 3 * 128, 128)]
+            src = fin1.at[(i - 9) // 3, :, pl.ds((i - 9) % 3 * 128, 128)]
         cgo[i // OT, :, pl.ds((i % OT) * 128, 128)] = src[...]
     load(cgo, cg_hbm).wait()
 
@@ -524,13 +565,14 @@
         scratch_shapes=[
             v((C, T), BF16), v((2, O, 128), BF16), v((2, 16, O), BF16), v((4, 32, O), BF16), v((2, 16, O), BF16),
             v((C, N), BF16), v((4, O), F32), v((4 * O, Q), BF16), v((R, O), BF16),
-            v((TB, C), BF16), v((N // 128, T + 16, 128), F32), v((OT, T + 16, 128), F32), v((T, N), BF16),
+            v((TC, C), BF16), v((N // 128, T + 16, 128), F32), v((OT, T + 16, 128), F32), v((T, N), BF16),
             v((4, R, O), BF16), v((R, 4 * O), BF16), v((R, Q), BF16),
             v((4, XB, COLS[0]), BF16), v((4, XB, COLS[0]), BF16), v((4, XB, COLS[0]), BF16),
             v((XB // 2, COLS[0]), BF16), v((XB // 2, COLS[0]), BF16), v((XB, COLS[0]), BF16), v((XB, COLS[0]), BF16),
-            v((4, 2, ZB, PIECE[0]), BF16), v((4, XB, PIECE[0]), BF16), v((4, XB, PIECE[0]), BF16), v((XB, PIECE[1]), BF16),
-            v((48, PIECE[1]), BF16), v((32, PIECE[1]), BF16), v((ZB, PIECE[1]), BF16), v((ZB, PIECE[1]), BF16),
-            v((2, 2, ZB, PIECE[0]), BF16), v((KW, ZB, O), BF16),
+            v((4, ZB, COLS[0]), BF16), v((2, 4, ZB, COLS[0]), BF16), v((2, 3, ZB, COLS[0]), BF16),
+            v((2, 4, XB, PIECE), BF16), v((XB, PIECE), BF16),
+            v((48, PIECE), BF16), v((32, PIECE), BF16), v((ZB, PIECE), BF16), v((ZB, PIECE), BF16),
+            v((ZB, COLS[0]), BF16), v((2, ZB, PIECE), BF16), v((KW, ZB, O), BF16),
             pltpu.SemaphoreType.DMA((16,)), pltpu.SemaphoreType.DMA((COPIES,)), pltpu.SemaphoreType.DMA((COPIES,)),
         ],
         compiler_params=pltpu.CompilerParams(collective_id=0, has_side_effects=True, vmem_limit_bytes=58 * 2**20),

time: 91.8 us -> 85.9 us (0.936)
  Pallas kernels: 90.9 us -> 85 us
    pallas_call x1, Pallas kernels: 88.8 us -> 82.9 us  [on_device(): pl.pallas_call(kernel, name='block', out_shape=(jax.ShapeDtypeStruct((R,...]
where the time goes in v3:
time: 85.9 us; the launch traced here: 85.8 us
  Pallas kernels  85 us (99%)
    pallas_call x1, Pallas kernels, on_device(): pl.pallas_call(kernel, name='block', out_shape=(jax.ShapeDtypeStruct((R,...  82.9 us
    pallas_call x1, Pallas kernels, on_device(): pl.pallas_call(finish, name='finish', out_shape=(jax.ShapeDtypeStruct((R,...  2.08 us

profile of v3, /device:TPU:1, one launch (start us, length us, event | category | flops | bytes accessed | tf_op | source)
XLA Modules:
  0.0 85.8 jit_solution(9438165140759174139)
XLA Ops:
  0.6 82.9 %block.1 = (bf16[512,640]{1,0:T(8,128)(2,1)}, bf16[5,80,384]{2,1,0:T(8,128)(2,1)}) custom-call(bf16[320,1024]{1,0:T(8,128)(2,1)} %bitcast.6, bf16[5,1280,384]{2,1,0:T(8,128)(2,1)} %w_hbm.1, f32[384]{0:T(512)} %gain_hbm.1, bf16[1536,640]{1,0:T(8,128)(2,1)} %qw_hbm.1, bf16[512,384]{1,0:T(8,128)(2,1)} %bitcast.7), custom_call_target="tpu_custom_call" | custom-call | tf_op jit(solution)/shard_map/block/pallas_call | solution.py:559
  83.5 2.1 %finish.1 = (bf16[512,640]{1,0:T(8,128)(2,1)}, f32[5,80,384]{2,1,0:T(8,128)}) custom-call(bf16[512,640]{1,0:T(8,128)(2,1)} %get-tuple-element.6.qkv_in, bf16[5,80,384]{2,1,0:T(8,128)(2,1)} %get-tuple-element.7.grad_in), custom_call_target="tpu_custom_call" | custom-call | tf_op jit(solution)/shard_map/finish/pallas_call | solution.py:580

commit v4 on v3

--- a/solution.py
+++ b/solution.py
@@ -28,16 +28,17 @@
 EDGE_UP, EDGE_DOWN, GRAD_UP, GRAD_DOWN, RIM, GAIN = 32, 33, 34, 35, 35, 38
 ENC_R, ENC_L, EFWD_R, EFWD_L = 42, 44, 46, 47
 SWAP = 48
-X1R, X1L, X2R, X2L = 52, 53, 54, 56
-ZUA, ZUB, ZDA, ZDB = 58, 62, 66, 70
-DUP, DDN, DSW = 74, 75, 76
-COPIES = 78
+SPLIT = (0, 4)
+X1R, X1L, X2R, X2L = 53, 54, 55, 57
+ZUA, ZUB, ZDA, ZDB = 59, 63, 67, 71
+DUP, DDN, DSW = 75, 76, 77
+COPIES = 79
 
 
 def kernel(
-    xt_hbm, w_hbm, gain_hbm, qw_hbm, eg_hbm, qkv_hbm, cg_hbm,
-    xt, ends, edge, rim, egrim, wcat, gain, qw, eg, xrow, yb, pgb, pgcat, enc, norm, qout,
-    psend, precv, gown, x1l, x1r, x2l, x2r, zb, zr, zs, zr1, zs1, u1l, u1r, u2l, u2r, fin0, fin1, cgo,
+    xt_hbm, w_hbm, gain_hbm, qw_hbm, eg_hbm, qout, cgo,
+    xt, ends, edge, rim, egrim, wcat, gain, qw, eg, xrow, yb, pgb, pgcat, enc, norm,
+    psend, precv, gown, x1l, x1r, x2l, x2r, zb, zr, zs, zr1, zs1, u1l, u1r, u2l, u2r, fin0, fin1,
     lsem, ssem, rsem,
 ):
     seq, mp, dp = lax.axis_index("seq"), lax.axis_index("mp"), lax.axis_index("dp")
@@ -276,9 +277,6 @@
     send(half_rows(mp, 0), half_rows(mp, 0), ENC_L, y_left)
     gradient_columns(384, 640)
 
-    def rows_of_x(xb):
-        return xt[pl.ds(pl.multiple_of(xb * XB, XB), XB), :]
-
     def rows_of_z(g):
         return jnp.concatenate(
             [xt[pl.ds(pl.multiple_of(xb * XB + g * ZB, ZB), ZB), :] for xb in range(4)], axis=0
@@ -297,22 +295,35 @@
             lane = width // 256 * 256
             write(lane, 128, jnp.dot(left, pgcat[:, pl.ds(first + lane, 128)], preferred_element_type=F32))
 
-    def theirs(other, step, b):
+    def left_rows(kind, b, half):
+        if kind:
+            return rows_of_z(b)
+        first, rows = (0, XB) if half is None else (half * (XB // 2), XB // 2)
+        return xt[pl.ds(pl.multiple_of(b * XB + first, XB // 2), rows), :]
+
+    def span(half):
+        return pl.ds(0, XB) if half is None else pl.ds(half * (XB // 2), XB // 2)
+
+    def theirs(other, step, b, half=None):
+        rows = span(half)
+
         def write(lane, width, value):
-            psend[b, :, pl.ds(lane, width)] = value.astype(BF16)
-
-        products((rows_of_z if other else rows_of_x)(b), other, write)
+            psend[b, rows, pl.ds(lane, width)] = value.astype(BF16)
+
+        products(left_rows(other, b, half), other, write)
         cols = pl.ds(0, COLS[other])
-        send(psend.at[b, :, cols], precv.at[b, :, cols], SWAP + step, partner)
-
-    def ours(me, step, b):
-        arrived(precv.at[b, :, pl.ds(0, COLS[me])], SWAP + step)
+        send(psend.at[b, rows, cols], precv.at[b, rows, cols], SWAP + step, partner)
+
+    def ours(me, step, b, half=None, waits=True):
+        rows = span(half)
+        if waits:
+            arrived(precv.at[b, span(half if me == 0 and step in SPLIT else None), pl.ds(0, COLS[me])], SWAP + step)
 
         def write(lane, width, value):
             cols = pl.ds(lane, width)
-            gown[b, :, cols] = (value + precv[b, :, cols].astype(F32)).astype(BF16)
-
-        products((rows_of_z if me else rows_of_x)(b), me, write)
+            gown[b, rows, cols] = (value + precv[b, rows, cols].astype(F32)).astype(BF16)
+
+        products(left_rows(me, b, half), me, write)
 
     def add(dst, src):
         for r in range(0, dst.shape[0], 16):
@@ -390,15 +401,17 @@
     @pl.when(core == 0)
     def _():
         theirs(1, 0, gf)
+        ours(0, 0, xf, 0)
+        send(gown.at[xf, top], x1l, X1R, x_right)
+        ours(0, 4, xf, 1)
+        send(gown.at[xf, bottom], x1r, X1L, x_left)
         theirs(1, 1, gr)
+        ours(0, 1, xr, 1)
+        send(gown.at[xr, bottom], x2l.at[bottom], X2R + 1, x_right)
+        ours(0, 1, xr, 0, waits=False)
         theirs(1, 2, gl)
-        ours(0, 0, xf)
-        send(gown.at[xf, top], x1l, X1R, x_right)
-        send(gown.at[xf, bottom], x1r, X1L, x_left)
+        forward_encoded()
         theirs(1, 3, zl)
-        ours(0, 1, xr)
-        send(gown.at[xr, bottom], x2l.at[bottom], X2R + 1, x_right)
-        forward_encoded()
         ours(0, 2, xl)
         send(gown.at[xl, top], x2r.at[top], X2L, x_left)
         arrived(x1l, X1R)
@@ -409,7 +422,8 @@
         send(gown.at[xl, bottom], x2r.at[bottom], X2L + 1, x_left)
         ours(0, 3, x)
         encoded_complete()
-        heads(0)
+        for part in range(4):
+            heads(part)
         for half, rows in ((0, top), (1, bottom)):
             arrived(x2l.at[rows], X2R + half)
             arrived(x2r.at[rows], X2L + half)
@@ -436,14 +450,10 @@
 
         z_chain(1, 0, base, received, staged)
         z_chain(2, 1, base, received, staged)
-        heads(1)
         z_chain(2, 0, base, received, staged)
         z_chain(3, 1, base, received, staged)
-        heads(2)
         z_chain(3, 0, base, received, staged)
         z_chain(4, 1, base, received, staged)
-        heads(3)
-        load(qout, qkv_hbm)
         z_chain(4, 0, base, received, staged)
         z_last(received)
         add3(fin0, zb.at[zl], zr.at[0, 3], zr.at[1, 3])
@@ -452,12 +462,12 @@
         arrived(fin1.at[upper], DSW + 1)
         for copy in sent:
             copy.wait_send()
-        local[-1].wait()
 
     @pl.when(core == 1)
     def _():
         del sent[shared:]
-        theirs(0, 0, xf)
+        theirs(0, 0, xf, 0)
+        theirs(0, 4, xf, 1)
         theirs(0, 1, xr)
         ours(1, 0, gf)
 
@@ -517,7 +527,6 @@
         send(mine, fin1.at[zh], DUP, z_up2)
         send(mine, fin1.at[zh], DDN, z_down2)
         heads(3)
-        load(qout, qkv_hbm)
         arrived(fin1.at[lower], DUP)
         send(fin1.at[lower], fin1.at[lower], DSW, partner)
         arrived(fin1.at[upper], DDN)
@@ -525,31 +534,24 @@
         arrived(fin0, DSW)
         for copy in sent:
             copy.wait_send()
-        local[-1].wait()
 
     for i in range(N // 128):
         if i < 9:
             src = fin0.at[:, pl.ds(i * 128, 128)]
         else:
             src = fin1.at[(i - 9) // 3, :, pl.ds((i - 9) % 3 * 128, 128)]
-        cgo[i // OT, :, pl.ds((i % OT) * 128, 128)] = src[...]
-    load(cgo, cg_hbm).wait()
-
-
-def finish(qkv_in, grad_in, qkv_out, grad_out, qkv, grad, wide, sem):
-    first = pltpu.make_async_copy(grad_in, grad, sem.at[0])
-    second = pltpu.make_async_copy(qkv_in, qkv, sem.at[1])
-    first.start()
-    second.start()
-    first.wait()
-    wide[...] = grad[...].astype(F32)
-    third = pltpu.make_async_copy(wide, grad_out, sem.at[2])
-    third.start()
-    second.wait()
-    fourth = pltpu.make_async_copy(qkv, qkv_out, sem.at[3])
-    fourth.start()
-    third.wait()
-    fourth.wait()
+        cgo[i // OT, :, pl.ds((i % OT) * 128, 128)] = src[...].astype(F32)
+
+
+def finish(qkv_in, grad_in, qkv_out, grad_out, sem):
+    copies = [
+        pltpu.make_async_copy(grad_in, grad_out, sem.at[0]),
+        pltpu.make_async_copy(qkv_in, qkv_out, sem.at[1]),
+    ]
+    for copy in copies:
+        copy.start()
+    for copy in copies:
+        copy.wait()
 
 
 def on_device(block_input, conv_weight, norm_gain, qkv_weight, encoder_grad):
@@ -559,31 +561,32 @@
     qkv, grad = pl.pallas_call(
         kernel,
         name="block",
-        out_shape=(jax.ShapeDtypeStruct((R, Q), BF16), jax.ShapeDtypeStruct((KW, ZB, O), BF16)),
-        in_specs=[any_] * 5,
-        out_specs=(any_, any_),
+        out_shape=(jax.ShapeDtypeStruct((R, Q), BF16), jax.ShapeDtypeStruct((KW, ZB, O), F32)),
+        in_specs=[pl.BlockSpec(memory_space=pltpu.HBM)] * 5,
+        out_specs=(pl.BlockSpec(memory_space=pltpu.VMEM),) * 2,
         scratch_shapes=[
             v((C, T), BF16), v((2, O, 128), BF16), v((2, 16, O), BF16), v((4, 32, O), BF16), v((2, 16, O), BF16),
             v((C, N), BF16), v((4, O), F32), v((4 * O, Q), BF16), v((R, O), BF16),
             v((TC, C), BF16), v((N // 128, T + 16, 128), F32), v((OT, T + 16, 128), F32), v((T, N), BF16),
-            v((4, R, O), BF16), v((R, 4 * O), BF16), v((R, Q), BF16),
+            v((4, R, O), BF16), v((R, 4 * O), BF16),
             v((4, XB, COLS[0]), BF16), v((4, XB, COLS[0]), BF16), v((4, XB, COLS[0]), BF16),
             v((XB // 2, COLS[0]), BF16), v((XB // 2, COLS[0]), BF16), v((XB, COLS[0]), BF16), v((XB, COLS[0]), BF16),
             v((4, ZB, COLS[0]), BF16), v((2, 4, ZB, COLS[0]), BF16), v((2, 3, ZB, COLS[0]), BF16),
             v((2, 4, XB, PIECE), BF16), v((XB, PIECE), BF16),
             v((48, PIECE), BF16), v((32, PIECE), BF16), v((ZB, PIECE), BF16), v((ZB, PIECE), BF16),
-            v((ZB, COLS[0]), BF16), v((2, ZB, PIECE), BF16), v((KW, ZB, O), BF16),
+            v((ZB, COLS[0]), BF16), v((2, ZB, PIECE), BF16),
             pltpu.SemaphoreType.DMA((16,)), pltpu.SemaphoreType.DMA((COPIES,)), pltpu.SemaphoreType.DMA((COPIES,)),
         ],
-        compiler_params=pltpu.CompilerParams(collective_id=0, has_side_effects=True, vmem_limit_bytes=58 * 2**20),
-    )(xin.T, conv_weight, norm_gain, qkv_weight, eg)
+        compiler_params=pltpu.CompilerParams(collective_id=0, has_side_effects=True, vmem_limit_bytes=50 * 2**20),
+    )(*(pltpu.with_memory_space_constraint(a, pltpu.HBM) for a in (xin.T, conv_weight, norm_gain, qkv_weight, eg)))
     qkv, grad = pl.pallas_call(
         finish,
         name="finish",
         out_shape=(jax.ShapeDtypeStruct((R, Q), BF16), jax.ShapeDtypeStruct((KW, ZB, O), F32)),
         in_specs=[any_] * 2,
         out_specs=(any_, any_),
-        scratch_shapes=[v((R, Q), BF16), v((KW, ZB, O), BF16), v((KW, ZB, O), F32), pltpu.SemaphoreType.DMA((4,))],
+        scratch_shapes=[pltpu.SemaphoreType.DMA((2,))],
+        compiler_params=pltpu.CompilerParams(vmem_limit_bytes=4 * 2**20),
     )(qkv, grad)
     return qkv[None], grad.transpose(1, 0, 2)
 

time: 85.9 us -> 84.9 us (0.988)
  Pallas kernels: 85 us -> 84.1 us
    pallas_call x1, Pallas kernels: 2.08 us -> 1.06 us  [on_device(): pl.pallas_call(finish, name='finish', out_shape=(jax.ShapeDtypeStruct((R,...]
where the time goes in v4:
time: 84.9 us
  Pallas kernels  84.1 us (99%)
    pallas_call x1, Pallas kernels, on_device(): pl.pallas_call(kernel, name='block', out_shape=(jax.ShapeDtypeStruct((R,...  83 us

profile of v4, /device:TPU:1, one launch (start us, length us, event | category | flops | bytes accessed | tf_op | source)
XLA Modules:
  0.0 84.9 jit_solution(9384398310480598452)
XLA Ops:
  0.6 83.0 %block.1 = (bf16[512,640]{1,0:T(8,128)(2,1)S(1)}, f32[5,80,384]{2,1,0:T(8,128)S(1)}) custom-call(bf16[320,1024]{1,0:T(8,128)(2,1)} %bitcast.6, bf16[5,1280,384]{2,1,0:T(8,128)(2,1)} %w_hbm.1, f32[384]{0:T(512)} %gain_hbm.1, bf16[1536,640]{1,0:T(8,128)(2,1)} %qw_hbm.1, bf16[512,384]{1,0:T(8,128)(2,1)} %bitcast.7), custom_call_target="tpu_custom_call" | custom-call | tf_op jit(solution)/shard_map/block/pallas_call | solution.py:561
  83.6 1.1 %finish.1 = (bf16[512,640]{1,0:T(8,128)(2,1)}, f32[5,80,384]{2,1,0:T(8,128)}) custom-call(bf16[512,640]{1,0:T(8,128)(2,1)S(1)} %get-tuple-element.6.qkv_in, f32[5,80,384]{2,1,0:T(8,128)S(1)} %get-tuple-element.7.grad_in), custom_call_target="tpu_custom_call" | custom-call | tf_op jit(solution)/shard_map/finish/pallas_call | solution.py:582

commit v5 on v4

--- a/solution.py
+++ b/solution.py
@@ -20,8 +20,8 @@
 TC = 256
 XB = 320
 ZB = 80
-COLS = (9 * 128, 6 * 128)
-PIECE = 3 * 128
+COLS = (7 * 128, 8 * 128)
+PIECE = 4 * 128
 Y0 = 8
 
 OWN_R, OWN_L, FWD_R, FWD_L = 0, 8, 16, 24
@@ -372,7 +372,7 @@
         rows = pl.ds(part * 128, 128)
         qout[rows, :] = jnp.dot(norm[rows, :], qw[...], preferred_element_type=F32).astype(BF16)
 
-    top, bottom = pl.ds(0, XB // 2), pl.ds(XB // 2, XB // 2)
+    top, bottom, own = pl.ds(0, XB // 2), pl.ds(XB // 2, XB // 2), pl.ds(0, COLS[0])
     xf, xr, xl = (x + 2) % 4, (x + 1) % 4, (x + 3) % 4
     gf, gr, gl = (zl + 2) % 4, (zl + 1) % 4, (zl + 3) % 4
 
@@ -402,24 +402,24 @@
     def _():
         theirs(1, 0, gf)
         ours(0, 0, xf, 0)
-        send(gown.at[xf, top], x1l, X1R, x_right)
+        send(gown.at[xf, top, own], x1l, X1R, x_right)
         ours(0, 4, xf, 1)
-        send(gown.at[xf, bottom], x1r, X1L, x_left)
+        send(gown.at[xf, bottom, own], x1r, X1L, x_left)
         theirs(1, 1, gr)
         ours(0, 1, xr, 1)
-        send(gown.at[xr, bottom], x2l.at[bottom], X2R + 1, x_right)
+        send(gown.at[xr, bottom, own], x2l.at[bottom], X2R + 1, x_right)
         ours(0, 1, xr, 0, waits=False)
         theirs(1, 2, gl)
         forward_encoded()
         theirs(1, 3, zl)
         ours(0, 2, xl)
-        send(gown.at[xl, top], x2r.at[top], X2L, x_left)
+        send(gown.at[xl, top, own], x2r.at[top], X2L, x_left)
         arrived(x1l, X1R)
-        add(gown.at[xr, top], x1l)
-        send(gown.at[xr, top], x2l.at[top], X2R, x_right)
+        add(gown.at[xr, top, own], x1l)
+        send(gown.at[xr, top, own], x2l.at[top], X2R, x_right)
         arrived(x1r, X1L)
-        add(gown.at[xl, bottom], x1r)
-        send(gown.at[xl, bottom], x2r.at[bottom], X2L + 1, x_left)
+        add(gown.at[xl, bottom, own], x1r)
+        send(gown.at[xl, bottom, own], x2r.at[bottom], X2L + 1, x_left)
         ours(0, 3, x)
         encoded_complete()
         for part in range(4):
@@ -429,9 +429,9 @@
             arrived(x2r.at[rows], X2L + half)
         for g in range(4):
             rows = pl.ds(g * ZB, ZB)
-            add3(zb.at[g], gown.at[x, rows], x2l.at[rows], x2r.at[rows])
-
-        spans = (pl.ds(0, 640), pl.ds(640, 512))
+            add3(zb.at[g], gown.at[x, rows, own], x2l.at[rows], x2r.at[rows])
+
+        spans = (pl.ds(0, 512), pl.ds(512, 384))
 
         def cols(sign, part):
             return spans[part if sign == 1 else 1 - part]
@@ -536,10 +536,10 @@
             copy.wait_send()
 
     for i in range(N // 128):
-        if i < 9:
+        if i < 7:
             src = fin0.at[:, pl.ds(i * 128, 128)]
         else:
-            src = fin1.at[(i - 9) // 3, :, pl.ds((i - 9) % 3 * 128, 128)]
+            src = fin1.at[(i - 7) // 4, :, pl.ds((i - 7) % 4 * 128, 128)]
         cgo[i // OT, :, pl.ds((i % OT) * 128, 128)] = src[...].astype(F32)
 
 
@@ -569,7 +569,7 @@
             v((C, N), BF16), v((4, O), F32), v((4 * O, Q), BF16), v((R, O), BF16),
             v((TC, C), BF16), v((N // 128, T + 16, 128), F32), v((OT, T + 16, 128), F32), v((T, N), BF16),
             v((4, R, O), BF16), v((R, 4 * O), BF16),
-            v((4, XB, COLS[0]), BF16), v((4, XB, COLS[0]), BF16), v((4, XB, COLS[0]), BF16),
+            v((4, XB, COLS[1]), BF16), v((4, XB, COLS[1]), BF16), v((4, XB, COLS[1]), BF16),
             v((XB // 2, COLS[0]), BF16), v((XB // 2, COLS[0]), BF16), v((XB, COLS[0]), BF16), v((XB, COLS[0]), BF16),
             v((4, ZB, COLS[0]), BF16), v((2, 4, ZB, COLS[0]), BF16), v((2, 3, ZB, COLS[0]), BF16),
             v((2, 4, XB, PIECE), BF16), v((XB, PIECE), BF16),

time: 84.9 us -> 84.9 us (level)
  no operation moved by 1% of the time
where the time goes in v5:
time: 84.9 us; the launch traced here: 84.8 us
  Pallas kernels  84 us (99%)
    pallas_call x1, Pallas kernels, on_device(): pl.pallas_call(kernel, name='block', out_shape=(jax.ShapeDtypeStruct((R,...  82.9 us

profile of v5, /device:TPU:1, one launch (start us, length us, event | category | flops | bytes accessed | tf_op | source)
XLA Modules:
  0.0 84.8 jit_solution(10451865435900983476)
XLA Ops:
  0.6 82.9 %block.1 = (bf16[512,640]{1,0:T(8,128)(2,1)S(1)}, f32[5,80,384]{2,1,0:T(8,128)S(1)}) custom-call(bf16[320,1024]{1,0:T(8,128)(2,1)} %bitcast.6, bf16[5,1280,384]{2,1,0:T(8,128)(2,1)} %w_hbm.1, f32[384]{0:T(512)} %gain_hbm.1, bf16[1536,640]{1,0:T(8,128)(2,1)} %qw_hbm.1, bf16[512,384]{1,0:T(8,128)(2,1)} %bitcast.7), custom_call_target="tpu_custom_call" | custom-call | tf_op jit(solution)/shard_map/block/pallas_call | solution.py:561
  83.6 1.1 %finish.1 = (bf16[512,640]{1,0:T(8,128)(2,1)}, f32[5,80,384]{2,1,0:T(8,128)}) custom-call(bf16[512,640]{1,0:T(8,128)(2,1)S(1)} %get-tuple-element.6.qkv_in, f32[5,80,384]{2,1,0:T(8,128)S(1)} %get-tuple-element.7.grad_in), custom_call_target="tpu_custom_call" | custom-call | tf_op jit(solution)/shard_map/finish/pallas_call | solution.py:582

commit v6 on v5

--- a/solution.py
+++ b/solution.py
@@ -131,6 +131,7 @@
         edge[e] = ends[e].T[112 * e : 112 * e + 16, :]
     send(edge.at[1], rim.at[mp, pl.ds(0, 16)], EDGE_UP, s_up)
     send(edge.at[0], rim.at[mp, pl.ds(16, 16)], EDGE_DOWN, s_down)
+    send_own(2)
     own_x.wait()
 
     def tap_products(g, half):
@@ -224,8 +225,8 @@
 
     def serve(i):
         forward(i)
-        if i + 2 < T // TB:
-            send_own(i + 2)
+        if i + 3 < T // TB:
+            send_own(i + 3)
 
     def group(g):
         complete(2 * g)
@@ -262,6 +263,7 @@
     serve(7)
     tap_products(2, 1)
     activations(224, 128)
+    gradient_columns(384, 256)
     group(3)
     tap_products(3, 0)
     tap_products(3, 1)
@@ -275,7 +277,7 @@
     send(half_rows(mp, 1), half_rows(mp, 1), ENC_L + 1, y_left)
     send(half_rows(mp, 1), half_rows(mp, 1), ENC_R + 1, y_right)
     send(half_rows(mp, 0), half_rows(mp, 0), ENC_L, y_left)
-    gradient_columns(384, 640)
+    gradient_columns(640, 384)
 
     def rows_of_z(g):
         return jnp.concatenate(
@@ -412,11 +414,11 @@
         theirs(1, 2, gl)
         forward_encoded()
         theirs(1, 3, zl)
-        ours(0, 2, xl)
-        send(gown.at[xl, top, own], x2r.at[top], X2L, x_left)
         arrived(x1l, X1R)
         add(gown.at[xr, top, own], x1l)
         send(gown.at[xr, top, own], x2l.at[top], X2R, x_right)
+        ours(0, 2, xl)
+        send(gown.at[xl, top, own], x2r.at[top], X2L, x_left)
         arrived(x1r, X1L)
         add(gown.at[xl, bottom, own], x1r)
         send(gown.at[xl, bottom, own], x2r.at[bottom], X2L + 1, x_left)
@@ -492,10 +494,10 @@
         ours(1, 1, gr)
         hop(1, 2, 1)
         hop(1, 2, 0)
+        theirs(0, 3, x)
         ours(1, 2, gl)
         hop(-1, 2, 1)
         hop(-1, 2, 0)
-        theirs(0, 3, x)
         ours(1, 3, zl)
         z_chain(3, 1, base, received, base)
         z_chain(3, 0, base, received, base)

time: 84.9 us -> 84.6 us (level)
  no operation moved by 1% of the time
where the time goes in v6:
time: 84.6 us; the launch traced here: 84.5 us
  Pallas kernels  83.7 us (99%)
    pallas_call x1, Pallas kernels, on_device(): pl.pallas_call(kernel, name='block', out_shape=(jax.ShapeDtypeStruct((R,...  82.7 us

profile of v6, /device:TPU:1, one launch (start us, length us, event | category | flops | bytes accessed | tf_op | source)
XLA Modules:
  0.0 84.5 jit_solution(16708232707851852682)
XLA Ops:
  0.6 82.7 %block.1 = (bf16[512,640]{1,0:T(8,128)(2,1)S(1)}, f32[5,80,384]{2,1,0:T(8,128)S(1)}) custom-call(bf16[320,1024]{1,0:T(8,128)(2,1)} %bitcast.6, bf16[5,1280,384]{2,1,0:T(8,128)(2,1)} %w_hbm.1, f32[384]{0:T(512)} %gain_hbm.1, bf16[1536,640]{1,0:T(8,128)(2,1)} %qw_hbm.1, bf16[512,384]{1,0:T(8,128)(2,1)} %bitcast.7), custom_call_target="tpu_custom_call" | custom-call | tf_op jit(solution)/shard_map/block/pallas_call | solution.py:563
  83.3 1.1 %finish.1 = (bf16[512,640]{1,0:T(8,128)(2,1)}, f32[5,80,384]{2,1,0:T(8,128)}) custom-call(bf16[512,640]{1,0:T(8,128)(2,1)S(1)} %get-tuple-element.6.qkv_in, f32[5,80,384]{2,1,0:T(8,128)S(1)} %get-tuple-element.7.grad_in), custom_call_target="tpu_custom_call" | custom-call | tf_op jit(solution)/shard_map/finish/pallas_call | solution.py:584

commit v7 on v6

--- a/solution.py
+++ b/solution.py
@@ -22,6 +22,7 @@
 ZB = 80
 COLS = (7 * 128, 8 * 128)
 PIECE = 4 * 128
+REST = C - CB
 Y0 = 8
 
 OWN_R, OWN_L, FWD_R, FWD_L = 0, 8, 16, 24
@@ -37,7 +38,7 @@
 
 def kernel(
     xt_hbm, w_hbm, gain_hbm, qw_hbm, eg_hbm, qout, cgo,
-    xt, ends, edge, rim, egrim, wcat, gain, qw, eg, xrow, yb, pgb, pgcat, enc, norm,
+    xt, xown, ends, edge, rim, egrim, wcat, gain, qw, eg, xrow, yb, pgb, pgcat, enc, norm,
     psend, precv, gown, x1l, x1r, x2l, x2r, zb, zr, zs, zr1, zs1, u1l, u1r, u2l, u2r, fin0, fin1,
     lsem, ssem, rsem,
 ):
@@ -67,10 +68,18 @@
         local.append(copy)
         return copy
 
-    own_rows = pl.ds(pl.multiple_of(mp * CB, CB), CB)
+    own_rows = pl.ds(REST, CB)
     end_loads = [load(xt_hbm.at[:, pl.ds(e * (T - 128), 128)], ends.at[e, pl.ds(0, CB)]) for e in (0, 1)]
     own_x = load(xt_hbm, xt.at[own_rows])
-    loads = [load(w_hbm.at[k], wcat.at[:, pl.ds(k * O, O)]) for k in range(KW)]
+    own_again = load(xt_hbm, xown.at[pl.ds(0, CB)])
+    loads = [
+        load(
+            w_hbm.at[k, pl.ds(pl.multiple_of((mp + slot + 1) % 4 * CB, CB), CB)],
+            wcat.at[pl.ds(slot * CB, CB), pl.ds(k * O, O)],
+        )
+        for slot in (3, 0, 1, 2)
+        for k in range(KW)
+    ]
     eg_load = load(eg_hbm, eg)
     gain_load = load(gain_hbm, gain.at[mp])
     qw_load = load(qw_hbm, qw)
@@ -96,27 +105,28 @@
     def arrived(dst, i):
         remote(dst, dst, i, y_right).wait_recv()
 
-    def block(owner, half, tb):
-        first = owner * CB + (0 if half is None else half * (CB // 2))
+    def block(slot, half, tb):
+        first = slot * CB + (0 if half is None else half * (CB // 2))
         size = CB if half is None else CB // 2
-        return xt.at[pl.ds(pl.multiple_of(first, CB // 2), size), pl.ds(tb * TB, TB)]
+        return xt.at[pl.ds(first, size), pl.ds(tb * TB, TB)]
 
     m_left, m_right, m_far = (mp + 3) % 4, (mp + 1) % 4, (mp + 2) % 4
+    RIGHT, FAR, LEFT = 0, 1, 2
 
     def send_own(tb):
         src = xt_hbm.at[:, pl.ds(tb * TB, TB)]
-        send(src, block(mp, None, tb), OWN_R + tb, y_right)
-        send(src, block(mp, None, tb), OWN_L + tb, y_left)
+        send(src, block(LEFT, None, tb), OWN_R + tb, y_right)
+        send(src, block(RIGHT, None, tb), OWN_L + tb, y_left)
 
     def forward(tb):
-        arrived(block(m_left, None, tb), OWN_R + tb)
-        send(block(m_left, 0, tb), block(m_left, 0, tb), FWD_R + tb, y_right)
-        arrived(block(m_right, None, tb), OWN_L + tb)
-        send(block(m_right, 1, tb), block(m_right, 1, tb), FWD_L + tb, y_left)
+        arrived(block(LEFT, None, tb), OWN_R + tb)
+        send(block(LEFT, 0, tb), block(FAR, 0, tb), FWD_R + tb, y_right)
+        arrived(block(RIGHT, None, tb), OWN_L + tb)
+        send(block(RIGHT, 1, tb), block(FAR, 1, tb), FWD_L + tb, y_left)
 
     def complete(tb):
-        arrived(block(m_far, 0, tb), FWD_R + tb)
-        arrived(block(m_far, 1, tb), FWD_L + tb)
+        arrived(block(FAR, 0, tb), FWD_R + tb)
+        arrived(block(FAR, 1, tb), FWD_L + tb)
 
     send_own(0)
     send_own(1)
@@ -133,24 +143,40 @@
     send(edge.at[0], rim.at[mp, pl.ds(16, 16)], EDGE_DOWN, s_down)
     send_own(2)
     own_x.wait()
+    own_again.wait()
+    xown[CB:, :] = jnp.zeros((O - CB, T), BF16)
+
+    def own_products(g):
+        xrow[:, :O] = xown[:, g * TC : (g + 1) * TC].T
+
+        def tile(n, carry):
+            cols = pl.ds(pl.multiple_of(n * 256, 256), 256)
+            y = jnp.dot(xrow[:, :CB], wcat[REST:, cols], preferred_element_type=F32)
+            yb[2 * n, pl.ds(Y0 + g * TC, TC), :] = y[:, :128]
+            yb[2 * n + 1, pl.ds(Y0 + g * TC, TC), :] = y[:, 128:]
+            return carry
+
+        lax.fori_loop(0, N // 256, tile, 0)
+        y = jnp.dot(xrow[:, :CB], wcat[REST:, N - 128 :], preferred_element_type=F32)
+        yb[N // 128 - 1, pl.ds(Y0 + g * TC, TC), :] = y
 
     def tap_products(g, half):
         if half == 0:
-            xrow[...] = xt[:, g * TC : (g + 1) * TC].T
+            xrow[...] = xt[:1024, g * TC : (g + 1) * TC].T
 
         def tile(n, carry):
             cols = pl.ds(pl.multiple_of(n * 256, 256), 256)
-            y = jnp.dot(xrow[...], wcat[:, cols], preferred_element_type=F32)
-            yb[2 * n, pl.ds(Y0 + g * TC, TC), :] = y[:, :128]
-            yb[2 * n + 1, pl.ds(Y0 + g * TC, TC), :] = y[:, 128:]
+            y = jnp.dot(xrow[:, :REST], wcat[:REST, cols], preferred_element_type=F32)
+            yb[2 * n, pl.ds(Y0 + g * TC, TC), :] += y[:, :128]
+            yb[2 * n + 1, pl.ds(Y0 + g * TC, TC), :] += y[:, 128:]
             return carry
 
         if half == 0:
             lax.fori_loop(0, 4, tile, 0)
         else:
             lax.fori_loop(4, N // 256, tile, 0)
-            y = jnp.dot(xrow[...], wcat[:, N - 128 :], preferred_element_type=F32)
-            yb[N // 128 - 1, pl.ds(Y0 + g * TC, TC), :] = y
+            y = jnp.dot(xrow[:, :REST], wcat[:REST, N - 128 :], preferred_element_type=F32)
+            yb[N // 128 - 1, pl.ds(Y0 + g * TC, TC), :] += y
 
     def rim_products():
         for d in (1, 2, 3):
@@ -159,16 +185,24 @@
         before = jnp.where(seq > 0, 1.0, 0.0).astype(F32)
         after = jnp.where(seq < 15, 1.0, 0.0).astype(F32)
 
+        def rims(cols, width):
+            y = jnp.zeros((32, width), F32)
+            for slot in range(4):
+                left = rim[(mp + slot + 1) % 4][:, :CB]
+                y += jnp.dot(left, wcat[slot * CB : (slot + 1) * CB, cols], preferred_element_type=F32)
+            return y[8:16] * before, y[16:24] * after
+
         def tile(n, carry):
-            cols = pl.ds(pl.multiple_of(n * 128, 128), 128)
-            y = jnp.zeros((32, 128), F32)
-            for m in range(4):
-                y += jnp.dot(rim[m][:, :CB], wcat[m * CB : (m + 1) * CB, cols], preferred_element_type=F32)
-            yb[n, pl.ds(0, 8), :] = y[8:16] * before
-            yb[n, pl.ds(Y0 + T, 8), :] = y[16:24] * after
+            first, last = rims(pl.ds(pl.multiple_of(n * 256, 256), 256), 256)
+            for i in range(2):
+                yb[2 * n + i, pl.ds(0, 8), :] = first[:, i * 128 : (i + 1) * 128]
+                yb[2 * n + i, pl.ds(Y0 + T, 8), :] = last[:, i * 128 : (i + 1) * 128]
             return carry
 
-        lax.fori_loop(0, N // 128, tile, 0)
+        lax.fori_loop(0, N // 256, tile, 0)
+        first, last = rims(pl.ds(N - 128, 128), 128)
+        yb[N // 128 - 1, pl.ds(0, 8), :] = first
+        yb[N // 128 - 1, pl.ds(Y0 + T, 8), :] = last
 
     def gelu(v):
         v2 = v * v
@@ -237,16 +271,22 @@
     arrived(rim.at[mp, pl.ds(16, 16)], EDGE_DOWN)
     for d in (1, 2, 3):
         send(rim.at[mp], rim.at[mp], RIM + d, at(m=(mp + d) % 4))
+    for copy in loads[:KW]:
+        copy.wait()
+    own_products(0)
     serve(1)
-    for copy in loads:
+    own_products(1)
+    serve(2)
+    own_products(2)
+    for copy in loads[KW:]:
         copy.wait()
-    serve(2)
     group(0)
     tap_products(0, 0)
     serve(3)
     tap_products(0, 1)
+    own_products(3)
+    serve(4)
     rim_products()
-    serve(4)
     group(1)
     tap_products(1, 0)
     serve(5)
@@ -281,7 +321,7 @@
 
     def rows_of_z(g):
         return jnp.concatenate(
-            [xt[pl.ds(pl.multiple_of(xb * XB + g * ZB, ZB), ZB), :] for xb in range(4)], axis=0
+            [xt[pl.ds(pl.multiple_of((xb - mp + 7) % 4 * XB + g * ZB, ZB), ZB), :] for xb in range(4)], axis=0
         )
 
     def products(left, owner, write):
@@ -301,7 +341,7 @@
         if kind:
             return rows_of_z(b)
         first, rows = (0, XB) if half is None else (half * (XB // 2), XB // 2)
-        return xt[pl.ds(pl.multiple_of(b * XB + first, XB // 2), rows), :]
+        return xt[pl.ds(pl.multiple_of((b - mp + 7) % 4 * XB + first, XB // 2), rows), :]
 
     def span(half):
         return pl.ds(0, XB) if half is None else pl.ds(half * (XB // 2), XB // 2)
@@ -567,9 +607,9 @@
         in_specs=[pl.BlockSpec(memory_space=pltpu.HBM)] * 5,
         out_specs=(pl.BlockSpec(memory_space=pltpu.VMEM),) * 2,
         scratch_shapes=[
-            v((C, T), BF16), v((2, O, 128), BF16), v((2, 16, O), BF16), v((4, 32, O), BF16), v((2, 16, O), BF16),
+            v((C, T), BF16), v((O, T), BF16), v((2, O, 128), BF16), v((2, 16, O), BF16), v((4, 32, O), BF16), v((2, 16, O), BF16),
             v((C, N), BF16), v((4, O), F32), v((4 * O, Q), BF16), v((R, O), BF16),
-            v((TC, C), BF16), v((N // 128, T + 16, 128), F32), v((OT, T + 16, 128), F32), v((T, N), BF16),
+            v((TC, 1024), BF16), v((N // 128, T + 16, 128), F32), v((OT, T + 16, 128), F32), v((T, N), BF16),
             v((4, R, O), BF16), v((R, 4 * O), BF16),
             v((4, XB, COLS[1]), BF16), v((4, XB, COLS[1]), BF16), v((4, XB, COLS[1]), BF16),
             v((XB // 2, COLS[0]), BF16), v((XB // 2, COLS[0]), BF16), v((XB, COLS[0]), BF16), v((XB, COLS[0]), BF16),
@@ -577,7 +617,7 @@
             v((2, 4, XB, PIECE), BF16), v((XB, PIECE), BF16),
             v((48, PIECE), BF16), v((32, PIECE), BF16), v((ZB, PIECE), BF16), v((ZB, PIECE), BF16),
             v((ZB, COLS[0]), BF16), v((2, ZB, PIECE), BF16),
-            pltpu.SemaphoreType.DMA((16,)), pltpu.SemaphoreType.DMA((COPIES,)), pltpu.SemaphoreType.DMA((COPIES,)),
+            pltpu.SemaphoreType.DMA((32,)), pltpu.SemaphoreType.DMA((COPIES,)), pltpu.SemaphoreType.DMA((COPIES,)),
         ],
         compiler_params=pltpu.CompilerParams(collective_id=0, has_side_effects=True, vmem_limit_bytes=50 * 2**20),
     )(*(pltpu.with_memory_space_constraint(a, pltpu.HBM) for a in (xin.T, conv_weight, norm_gain, qkv_weight, eg)))

time: 84.6 us -> 84.6 us (level)
  no operation moved by 1% of the time
where the time goes in v7:
time: 84.6 us; the launch traced here: 84.5 us
  Pallas kernels  83.7 us (99%)
    pallas_call x1, Pallas kernels, on_device(): pl.pallas_call(kernel, name='block', out_shape=(jax.ShapeDtypeStruct((R,...  82.7 us

profile of v7, /device:TPU:1, one launch (start us, length us, event | category | flops | bytes accessed | tf_op | source)
XLA Modules:
  0.0 84.5 jit_solution(9343022454144968757)
XLA Ops:
  0.6 82.7 %block.1 = (bf16[512,640]{1,0:T(8,128)(2,1)S(1)}, f32[5,80,384]{2,1,0:T(8,128)S(1)}) custom-call(bf16[320,1024]{1,0:T(8,128)(2,1)} %bitcast.6, bf16[5,1280,384]{2,1,0:T(8,128)(2,1)} %w_hbm.1, f32[384]{0:T(512)} %gain_hbm.1, bf16[1536,640]{1,0:T(8,128)(2,1)} %qw_hbm.1, bf16[512,384]{1,0:T(8,128)(2,1)} %bitcast.7), custom_call_target="tpu_custom_call" | custom-call | tf_op jit(solution)/shard_map/block/pallas_call | solution.py:603
  83.3 1.1 %finish.1 = (bf16[512,640]{1,0:T(8,128)(2,1)}, f32[5,80,384]{2,1,0:T(8,128)}) custom-call(bf16[512,640]{1,0:T(8,128)(2,1)S(1)} %get-tuple-element.6.qkv_in, f32[5,80,384]{2,1,0:T(8,128)S(1)} %get-tuple-element.7.grad_in), custom_call_target="tpu_custom_call" | custom-call | tf_op jit(solution)/shard_map/finish/pallas_call | solution.py:624

commit v8 on v6

--- a/solution.py
+++ b/solution.py
@@ -38,7 +38,7 @@
 def kernel(
     xt_hbm, w_hbm, gain_hbm, qw_hbm, eg_hbm, qout, cgo,
     xt, ends, edge, rim, egrim, wcat, gain, qw, eg, xrow, yb, pgb, pgcat, enc, norm,
-    psend, precv, gown, x1l, x1r, x2l, x2r, zb, zr, zs, zr1, zs1, u1l, u1r, u2l, u2r, fin0, fin1,
+    psend, precv, gown, x1l, x1r, x2l, x2r, zb, zr, zs, zr1, zs1, uf, u2l, u2r, fin0, fin1,
     lsem, ssem, rsem,
 ):
     seq, mp, dp = lax.axis_index("seq"), lax.axis_index("mp"), lax.axis_index("dp")
@@ -55,6 +55,7 @@
     y_right, y_left = at(m=(mp + 1) % 4), at(m=(mp + 3) % 4)
     s_up, s_down = at(s=(seq + 1) % 16), at(s=(seq + 15) % 16)
     x_right, x_left = at(s=(seq + 4) % 16), at(s=(seq + 12) % 16)
+    x_far = at(s=(seq + 8) % 16)
     z_up, z_down = z_at((z + 1) % 8), z_at((z + 7) % 8)
     partner = at(d=zh * 2 + 1 - core)
     z_up2, z_down2 = z_at((z + 2) % 8), z_at((z + 6) % 8)
@@ -76,7 +77,7 @@
     qw_load = load(qw_hbm, qw)
 
     barrier = pltpu.get_barrier_semaphore()
-    peers = [y_right, y_left, at(m=(mp + 2) % 4), s_up, s_down, x_right, x_left, z_up, z_down, z_up2, z_down2, partner]
+    peers = [y_right, y_left, at(m=(mp + 2) % 4), s_up, s_down, x_right, x_left, x_far, z_up, z_down, z_up2, z_down2, partner]
     for peer in peers:
         pl.semaphore_signal(barrier, inc=1, device_id=peer, device_id_type=MESH)
     pl.semaphore_wait(barrier, len(peers))
@@ -498,34 +499,33 @@
         ours(1, 2, gl)
         hop(-1, 2, 1)
         hop(-1, 2, 0)
+        forward_encoded()
         ours(1, 3, zl)
         z_chain(3, 1, base, received, base)
         z_chain(3, 0, base, received, base)
-        forward_encoded()
         z_chain(4, 1, base, received, base)
         z_chain(4, 0, base, received, base)
         encoded_complete()
         heads(0)
+        heads(1)
         z_last(received)
         add3(zs1, piece(z), zr1.at[0, 3], zr1.at[1, 3])
 
-        def rows_at(xb, first, rows):
-            return zs1.at[pl.ds(pl.multiple_of(xb * ZB + first, 16), rows)]
-
-        send(rows_at(xf, 0, 48), u1l, X1R, x_right)
-        send(rows_at(xf, 48, 32), u1r, X1L, x_left)
-        heads(1)
-        arrived(u1l, X1R)
-        add(rows_at(xr, 0, 48), u1l)
-        send(rows_at(xr, 0, ZB), u2l, X2R, x_right)
-        arrived(u1r, X1L)
-        add(rows_at(xl, 48, 32), u1r)
-        send(rows_at(xl, 0, ZB), u2r, X2L, x_left)
+        def rows_at(xb):
+            return zs1.at[pl.ds(pl.multiple_of(xb * ZB, ZB), ZB)]
+
+        send(rows_at(xf), uf, X1R, x_far)
+        send(rows_at(xr), u2l, X2R, x_right)
+        send(rows_at(xl), u2r, X2L, x_left)
         heads(2)
         arrived(u2l, X2R)
         arrived(u2r, X2L)
-        mine = rows_at(x, 0, ZB)
-        add3(mine, mine, u2l, u2r)
+        arrived(uf, X1R)
+        mine = rows_at(x)
+        for r in range(0, ZB, 16):
+            rows = pl.ds(r, 16)
+            parts = [ref[rows, :].astype(F32) for ref in (mine, u2l, u2r, uf)]
+            mine[rows, :] = (parts[0] + parts[1] + parts[2] + parts[3]).astype(BF16)
         send(mine, fin1.at[zh], DUP, z_up2)
         send(mine, fin1.at[zh], DDN, z_down2)
         heads(3)
@@ -575,7 +575,7 @@
             v((XB // 2, COLS[0]), BF16), v((XB // 2, COLS[0]), BF16), v((XB, COLS[0]), BF16), v((XB, COLS[0]), BF16),
             v((4, ZB, COLS[0]), BF16), v((2, 4, ZB, COLS[0]), BF16), v((2, 3, ZB, COLS[0]), BF16),
             v((2, 4, XB, PIECE), BF16), v((XB, PIECE), BF16),
-            v((48, PIECE), BF16), v((32, PIECE), BF16), v((ZB, PIECE), BF16), v((ZB, PIECE), BF16),
+            v((ZB, PIECE), BF16), v((ZB, PIECE), BF16), v((ZB, PIECE), BF16),
             v((ZB, COLS[0]), BF16), v((2, ZB, PIECE), BF16),
             pltpu.SemaphoreType.DMA((16,)), pltpu.SemaphoreType.DMA((COPIES,)), pltpu.SemaphoreType.DMA((COPIES,)),
         ],

time: 84.6 us -> 84.1 us (level)
  no operation moved by 1% of the time
where the time goes in v8:
time: 84.1 us; the launch traced here: 84 us
  Pallas kernels  83.2 us (99%)
    pallas_call x1, Pallas kernels, on_device(): pl.pallas_call(kernel, name='block', out_shape=(jax.ShapeDtypeStruct((R,...  82.1 us

profile of v8, /device:TPU:1, one launch (start us, length us, event | category | flops | bytes accessed | tf_op | source)
XLA Modules:
  0.0 84.0 jit_solution(4515960572090126310)
XLA Ops:
  0.6 82.1 %block.1 = (bf16[512,640]{1,0:T(8,128)(2,1)S(1)}, f32[5,80,384]{2,1,0:T(8,128)S(1)}) custom-call(bf16[320,1024]{1,0:T(8,128)(2,1)} %bitcast.6, bf16[5,1280,384]{2,1,0:T(8,128)(2,1)} %w_hbm.1, f32[384]{0:T(512)} %gain_hbm.1, bf16[1536,640]{1,0:T(8,128)(2,1)} %qw_hbm.1, bf16[512,384]{1,0:T(8,128)(2,1)} %bitcast.7), custom_call_target="tpu_custom_call" | custom-call | tf_op jit(solution)/shard_map/block/pallas_call | solution.py:563
  82.8 1.1 %finish.1 = (bf16[512,640]{1,0:T(8,128)(2,1)}, f32[5,80,384]{2,1,0:T(8,128)}) custom-call(bf16[512,640]{1,0:T(8,128)(2,1)S(1)} %get-tuple-element.6.qkv_in, f32[5,80,384]{2,1,0:T(8,128)S(1)} %get-tuple-element.7.grad_in), custom_call_target="tpu_custom_call" | custom-call | tf_op jit(solution)/shard_map/finish/pallas_call | solution.py:584

commit v9 on v8

--- a/solution.py
+++ b/solution.py
@@ -424,9 +424,6 @@
         add(gown.at[xl, bottom, own], x1r)
         send(gown.at[xl, bottom, own], x2r.at[bottom], X2L + 1, x_left)
         ours(0, 3, x)
-        encoded_complete()
-        for part in range(4):
-            heads(part)
         for half, rows in ((0, top), (1, bottom)):
             arrived(x2l.at[rows], X2R + half)
             arrived(x2r.at[rows], X2L + half)
@@ -453,11 +450,16 @@
 
         z_chain(1, 0, base, received, staged)
         z_chain(2, 1, base, received, staged)
+        encoded_complete()
+        heads(0)
         z_chain(2, 0, base, received, staged)
         z_chain(3, 1, base, received, staged)
+        heads(1)
         z_chain(3, 0, base, received, staged)
         z_chain(4, 1, base, received, staged)
+        heads(2)
         z_chain(4, 0, base, received, staged)
+        heads(3)
         z_last(received)
         add3(fin0, zb.at[zl], zr.at[0, 3], zr.at[1, 3])
         send(fin0, fin0, DSW, partner)

time: 84.1 us -> 84.4 us (level)
  no operation moved by 1% of the time
where the time goes in v9:
time: 84.4 us
  Pallas kernels  83.6 us (99%)
    pallas_call x1, Pallas kernels, on_device(): pl.pallas_call(kernel, name='block', out_shape=(jax.ShapeDtypeStruct((R,...  82.5 us

profile of v9, /device:TPU:1, one launch (start us, length us, event | category | flops | bytes accessed | tf_op | source)
XLA Modules:
  0.0 84.4 jit_solution(7402507250553545483)
XLA Ops:
  0.6 82.5 %block.1 = (bf16[512,640]{1,0:T(8,128)(2,1)S(1)}, f32[5,80,384]{2,1,0:T(8,128)S(1)}) custom-call(bf16[320,1024]{1,0:T(8,128)(2,1)} %bitcast.6, bf16[5,1280,384]{2,1,0:T(8,128)(2,1)} %w_hbm.1, f32[384]{0:T(512)} %gain_hbm.1, bf16[1536,640]{1,0:T(8,128)(2,1)} %qw_hbm.1, bf16[512,384]{1,0:T(8,128)(2,1)} %bitcast.7), custom_call_target="tpu_custom_call" | custom-call | tf_op jit(solution)/shard_map/block/pallas_call | solution.py:565
  83.1 1.1 %finish.1 = (bf16[512,640]{1,0:T(8,128)(2,1)}, f32[5,80,384]{2,1,0:T(8,128)}) custom-call(bf16[512,640]{1,0:T(8,128)(2,1)S(1)} %get-tuple-element.6.qkv_in, f32[5,80,384]{2,1,0:T(8,128)S(1)} %get-tuple-element.7.grad_in), custom_call_target="tpu_custom_call" | custom-call | tf_op jit(solution)/shard_map/finish/pallas_call | solution.py:586

commit v10 on v9

--- a/solution.py
+++ b/solution.py
@@ -414,7 +414,6 @@
         ours(0, 1, xr, 0, waits=False)
         theirs(1, 2, gl)
         forward_encoded()
-        theirs(1, 3, zl)
         arrived(x1l, X1R)
         add(gown.at[xr, top, own], x1l)
         send(gown.at[xr, top, own], x2l.at[top], X2R, x_right)
@@ -423,6 +422,7 @@
         arrived(x1r, X1L)
         add(gown.at[xl, bottom, own], x1r)
         send(gown.at[xl, bottom, own], x2r.at[bottom], X2L + 1, x_left)
+        theirs(1, 3, zl)
         ours(0, 3, x)
         for half, rows in ((0, top), (1, bottom)):
             arrived(x2l.at[rows], X2R + half)

time: 84.4 us -> 84.7 us (level)
  no operation moved by 1% of the time
where the time goes in v10:
time: 84.7 us; the launch traced here: 84.6 us
  Pallas kernels  83.8 us (99%)
    pallas_call x1, Pallas kernels, on_device(): pl.pallas_call(kernel, name='block', out_shape=(jax.ShapeDtypeStruct((R,...  82.8 us

profile of v10, /device:TPU:1, one launch (start us, length us, event | category | flops | bytes accessed | tf_op | source)
XLA Modules:
  0.0 84.6 jit_solution(1496834892754411226)
XLA Ops:
  0.6 82.8 %block.1 = (bf16[512,640]{1,0:T(8,128)(2,1)S(1)}, f32[5,80,384]{2,1,0:T(8,128)S(1)}) custom-call(bf16[320,1024]{1,0:T(8,128)(2,1)} %bitcast.6, bf16[5,1280,384]{2,1,0:T(8,128)(2,1)} %w_hbm.1, f32[384]{0:T(512)} %gain_hbm.1, bf16[1536,640]{1,0:T(8,128)(2,1)} %qw_hbm.1, bf16[512,384]{1,0:T(8,128)(2,1)} %bitcast.7), custom_call_target="tpu_custom_call" | custom-call | tf_op jit(solution)/shard_map/block/pallas_call | solution.py:565
  83.4 1.1 %finish.1 = (bf16[512,640]{1,0:T(8,128)(2,1)}, f32[5,80,384]{2,1,0:T(8,128)}) custom-call(bf16[512,640]{1,0:T(8,128)(2,1)S(1)} %get-tuple-element.6.qkv_in, f32[5,80,384]{2,1,0:T(8,128)S(1)} %get-tuple-element.7.grad_in), custom_call_target="tpu_custom_call" | custom-call | tf_op jit(solution)/shard_map/finish/pallas_call | solution.py:586
